TPU v7x, 32 devices: a whole 2x2x4 slice. The times are simulated.
32 devices in a mesh: group: 2 (over x), ctx: 8 (over z, y), tp: 2 (over core).
Axes of the slice: x: 2, y: 2, z: 4, core: 2. Of those that a mesh axis runs over, the one named last changes fastest.
Arguments:
- x_in: bfloat16 [4096, 4096], P(('group', 'ctx', 'tp')), parts along dimension 0, may hold values from -6 to 6
- b_in: bfloat16 [4096, 512], P(('group', 'ctx', 'tp')), parts along dimension 0, may hold values from -6 to 6
- c_in: bfloat16 [4096, 512], P(('group', 'ctx', 'tp')), parts along dimension 0, may hold values from -6 to 6
- z_in: bfloat16 [4096, 4096], P(('group', 'ctx', 'tp')), parts along dimension 0, may hold values from -6 to 6
- dt_raw: bfloat16 [4096, 64], P(('group', 'ctx', 'tp')), parts along dimension 0, may hold values from -3 to 3
- conv_x: float32 [4, 4096], replicated, may hold values from -3 to 3
- conv_b: float32 [4, 512], replicated, may hold values from -3 to 3
- conv_c: float32 [4, 512], replicated, may hold values from -3 to 3
- decay_rate: float32 [64], replicated, may hold values from 3e-05 to 0.06
- dt_bias: float32 [64], replicated, may hold values from -1.5 to -0.5
- skip_scale: float32 [64], replicated, may hold values from 0.5 to 1.5
- norm_gain: float32 [4096], replicated, may hold values from 0.1 to 1.9
- w_value: float32 [4096], replicated, may hold values from -0.4 to 0.4
- resets: int32 [4096], P(('group', 'ctx')), parts along dimension 0, may hold values 0 or 1
- bucket: int32 [4096], P(('group', 'ctx')), parts along dimension 0, may hold values from 0 to 255
- return_table: float32 [256], replicated, may hold values from -16 to 16
Outputs:
- values: float32 [4096], P(('group', 'ctx', 'tp')), parts along dimension 0
- grad_x: bfloat16 [4096, 4096], P(('group', 'ctx', 'tp')), parts along dimension 0
- grad_b: bfloat16 [4096, 512], P(('group', 'ctx', 'tp')), parts along dimension 0
- grad_c: bfloat16 [4096, 512], P(('group', 'ctx', 'tp')), parts along dimension 0
- grad_z: bfloat16 [4096, 4096], P(('group', 'ctx', 'tp')), parts along dimension 0
- grad_dt: bfloat16 [4096, 64], P(('group', 'ctx', 'tp')), parts along dimension 0
There are 2 independent parts, one for each index of `group`. A program takes and returns all parts, laid end to end along the dimension named above; an argument that names none is the same for every part. Nothing has to cross between parts.
All inputs are finite; a program needn't handle non-finite values. No bound on the sum of `resets` on one device may be relied on, other than what follows from the above.
Results may differ from a plain program's by a relative error of at most 0.0058.
Values may be sent and summed in bfloat16 or wider, within the bound.
A program may use at most 192 MiB of HBM per device.

v0:
```python
from functools import partial

import jax
import jax.numpy as jnp
from jax import lax
from jax.sharding import PartitionSpec as P

HEADS = 64
HEAD_DIM = 64
GROUPS = 4
BLOCK = 128


epsilon = 1e-05
highest = lax.Precision.HIGHEST


def from_behind(value, axis, steps):
    count = lax.axis_size(axis)
    initial, last = (max(0, -steps), min(count, count - steps))
    return lax.ppermute(value, axis, [(source, source + steps) for source in range(initial, last)])


def carried_in(part, axis, combine, identity, reverse):
    count = lax.axis_size(axis)
    place = lax.axis_index(axis)
    ahead = count - 1 - place if reverse else place
    gathered = jax.tree.map(lambda a: lax.all_gather(a, axis), part)
    state = jax.tree.map(lambda a, e: jnp.zeros_like(a) + jnp.asarray(e, a.dtype), part, identity)

    def one(turn, state):
        source = count - 1 - turn if reverse else turn
        return combine(
            state, jax.tree.map(lambda a: lax.dynamic_index_in_dim(a, source, 0, False), gathered)
        )

    return lax.fori_loop(0, ahead, one, state)


def round_keep(value):
    narrow = lax.optimization_barrier(value.astype(jnp.bfloat16))
    return value + lax.stop_gradient(narrow.astype(jnp.float32) - value)


def shift_rows(values, amount):
    filler = jnp.zeros((amount,) + values.shape[1:], values.dtype)
    return jnp.concatenate([filler, values[: values.shape[0] - amount]], axis=0)


def seen_resets(reset_real):
    second = jnp.maximum(reset_real, shift_rows(reset_real, 1))
    third = jnp.maximum(second, shift_rows(reset_real, 2))
    return (reset_real, second, third)


def conv_silu(extended, weight, seen_flags):
    row_count = extended.shape[0] - 3
    summed = weight[0][None, :] * extended[3:]
    for offset in range(1, 4):
        valid = 1.0 - seen_flags[offset - 1]
        summed = (
            summed
            + weight[offset][None, :]
            * extended[3 - offset : 3 - offset + row_count]
            * valid[:, None]
        )
    return round_keep(jax.nn.silu(summed))


def block_decays(dt_rows, decay_rate, reset_real):
    cumulative = jnp.cumsum(-dt_rows * decay_rate[None, :], axis=0)
    counts = jnp.cumsum(reset_real, axis=0)
    return (cumulative, counts)


def block_state(x_conv, b_conv, dt_rows, cumulative, counts, per_group):
    row_count, head_count = dt_rows.shape
    alive = jnp.where(counts == counts[-1], 1.0, 0.0)
    weight_end = jnp.exp(cumulative[-1][None, :] - cumulative) * alive[:, None] * dt_rows
    x_heads = x_conv.reshape(row_count, head_count, -1) * weight_end[:, :, None]
    b_heads = jnp.repeat(b_conv.reshape(row_count, head_count // per_group, -1), per_group, axis=1)
    state_add = jnp.einsum("shp,shn->hpn", x_heads, b_heads, precision=highest)
    block_decay = jnp.exp(cumulative[-1]) * jnp.where(counts[-1] == 0.0, 1.0, 0.0)
    return (state_add, block_decay)


def block_output(x_conv, b_conv, c_conv, dt_rows, cumulative, counts, start_state, per_group):
    row_count, head_count = dt_rows.shape
    group_count = head_count // per_group
    b_groups = b_conv.reshape(row_count, group_count, -1)
    c_groups = c_conv.reshape(row_count, group_count, -1)
    scores = jnp.einsum("tgn,sgn->gts", c_groups, b_groups, precision=highest)
    rows_iota = lax.broadcasted_iota(jnp.int32, (row_count, row_count), 0)
    cols_iota = lax.broadcasted_iota(jnp.int32, (row_count, row_count), 1)
    same_seg = (rows_iota >= cols_iota) & (counts[:, None] == counts[None, :])
    log_gap = cumulative.T[:, :, None] - cumulative.T[:, None, :]
    fading = jnp.where(same_seg[None], jnp.exp(jnp.minimum(log_gap, 0.0)), 0.0)
    mixing = jnp.repeat(scores, per_group, axis=0) * fading * dt_rows.T[:, None, :]
    within = jnp.einsum(
        "hts,shp->thp", mixing, x_conv.reshape(row_count, head_count, -1), precision=highest
    )
    c_heads = jnp.repeat(c_groups, per_group, axis=1)
    carried = jnp.einsum("thn,hpn->thp", c_heads, start_state, precision=highest)
    reach_decay = jnp.exp(cumulative) * jnp.where(counts == 0.0, 1.0, 0.0)[:, None]
    return (within + carried * reach_decay[:, :, None]).reshape(row_count, -1)


def split_blocks(array, block_len):
    return array.reshape((array.shape[0] // block_len, block_len) + array.shape[1:])


def local_states(
    x_real,
    b_real,
    c_real,
    dt_real,
    tail_x,
    tail_b,
    tail_c,
    conv_x,
    conv_b,
    conv_c,
    decay_rate,
    dt_bias,
    reset_real,
    seen_flags,
    per_group,
    block_len,
):
    x_conv = conv_silu(jnp.concatenate([tail_x, x_real], axis=0), conv_x, seen_flags)
    b_conv = conv_silu(jnp.concatenate([tail_b, b_real], axis=0), conv_b, seen_flags)
    c_conv = conv_silu(jnp.concatenate([tail_c, c_real], axis=0), conv_c, seen_flags)
    dt_rows = jax.nn.softplus(dt_real + dt_bias[None, :])
    head_count = dt_rows.shape[1]
    head_width = x_conv.shape[1] // head_count
    state_width = b_conv.shape[1] * per_group // head_count

    def advance(state_now, pieces):
        x_piece, b_piece, dt_piece, reset_piece = pieces
        cumulative, counts = block_decays(dt_piece, decay_rate, reset_piece)
        state_add, block_decay = block_state(
            x_piece, b_piece, dt_piece, cumulative, counts, per_group
        )
        return (block_decay[:, None, None] * state_now + state_add, (state_now, block_decay))

    initial = jnp.zeros((head_count, head_width, state_width), jnp.float32)
    pieces = (
        split_blocks(x_conv, block_len),
        split_blocks(b_conv, block_len),
        split_blocks(dt_rows, block_len),
        split_blocks(reset_real, block_len),
    )
    end_state, (starts, decays) = lax.scan(advance, initial, pieces)
    return (x_conv, b_conv, c_conv, dt_rows, starts, end_state, jnp.prod(decays, axis=0))


def local_mix(
    x_conv,
    b_conv,
    c_conv,
    dt_rows,
    gate_real,
    starts,
    state_in,
    decay_rate,
    skip_scale,
    reset_real,
    per_group,
    block_len,
):
    row_count, head_count = dt_rows.shape
    emit = jax.checkpoint(partial(block_output, per_group=per_group))

    def advance(carry_decay, pieces):
        x_piece, b_piece, c_piece, dt_piece, reset_piece, start_piece = pieces
        cumulative, counts = block_decays(dt_piece, decay_rate, reset_piece)
        output = emit(
            x_piece,
            b_piece,
            c_piece,
            dt_piece,
            cumulative,
            counts,
            start_piece + carry_decay[:, None, None] * state_in,
        )
        block_decay = jnp.exp(cumulative[-1]) * jnp.where(counts[-1] == 0.0, 1.0, 0.0)
        return (carry_decay * block_decay, output)

    pieces = (
        split_blocks(x_conv, block_len),
        split_blocks(b_conv, block_len),
        split_blocks(c_conv, block_len),
        split_blocks(dt_rows, block_len),
        split_blocks(reset_real, block_len),
        starts,
    )
    _, outputs = lax.scan(advance, jnp.ones((head_count,), jnp.float32), pieces)
    mixed = outputs.reshape(row_count, head_count, -1) + skip_scale[None, :, None] * x_conv.reshape(
        row_count, head_count, -1
    )
    return mixed.reshape(row_count, -1) * jax.nn.silu(gate_real)


def link_pairs(earlier, later):
    return (earlier[0] * later[0], later[0][:, None, None] * earlier[1] + later[1])


def pair_identity(decays, states):
    return (jnp.ones_like(decays), jnp.zeros_like(states))


def layer_pass(
    x_rows,
    b_rows,
    c_rows,
    z_rows,
    dt_in,
    reset_rows,
    bucket_rows,
    conv_x,
    conv_b,
    conv_c,
    decay_rate,
    dt_bias,
    skip_scale,
    gain_weight,
    table,
    send_tails,
    carry_forward,
    carry_backward,
    return_tails,
    value_of,
):
    x_width = x_rows.shape[1]
    b_width = b_rows.shape[1]
    reset_real = reset_rows.astype(jnp.float32)
    keep_rows = jnp.stack(
        [
            1.0 - jnp.maximum(reset_real[-2], reset_real[-1]),
            1.0 - reset_real[-1],
            jnp.ones((), jnp.float32),
        ]
    )
    keep_narrow = keep_rows.astype(jnp.bfloat16)[:, None]
    outgoing = jnp.concatenate([x_rows[-3:], b_rows[-3:], c_rows[-3:]], axis=1) * keep_narrow
    incoming = send_tails(outgoing).astype(jnp.float32)
    seen_flags = seen_resets(reset_real)
    per_group = HEADS // GROUPS
    first_pass = partial(
        local_states,
        conv_x=conv_x,
        conv_b=conv_b,
        conv_c=conv_c,
        decay_rate=decay_rate,
        dt_bias=dt_bias,
        reset_real=reset_real,
        seen_flags=seen_flags,
        per_group=per_group,
        block_len=BLOCK,
    )
    states_out, pull_states = jax.vjp(
        first_pass,
        x_rows.astype(jnp.float32),
        b_rows.astype(jnp.float32),
        c_rows.astype(jnp.float32),
        dt_in.astype(jnp.float32),
        incoming[:, :x_width],
        incoming[:, x_width : x_width + b_width],
        incoming[:, x_width + b_width :],
    )
    x_conv, b_conv, c_conv, dt_rows, starts, end_state, device_decay = states_out
    state_in = carry_forward(device_decay, end_state)
    second_pass = partial(
        local_mix,
        decay_rate=decay_rate,
        skip_scale=skip_scale,
        reset_real=reset_real,
        per_group=per_group,
        block_len=BLOCK,
    )
    gated, pull_mix = jax.vjp(
        second_pass, x_conv, b_conv, c_conv, dt_rows, z_rows.astype(jnp.float32), starts, state_in
    )
    values, norm_rms = value_of(gated, gain_weight)
    onehot = jnp.where(
        bucket_rows[:, None] == lax.broadcasted_iota(jnp.int32, (1, table.shape[0]), 1), 1.0, 0.0
    )
    target = jnp.dot(onehot, table, precision=highest)
    value_grad = values - target
    width_all = HEADS * HEAD_DIM
    gated_grad = (value_grad / norm_rms)[:, None] * (
        gain_weight[None, :] - (values / (norm_rms * width_all))[:, None] * gated
    )
    mix_grads = pull_mix(gated_grad)
    state_grad = carry_backward(device_decay, mix_grads[6])
    decay_grad = jnp.sum(state_grad * state_in, axis=(1, 2))
    in_grads = pull_states(
        (
            mix_grads[0],
            mix_grads[1],
            mix_grads[2],
            mix_grads[3],
            mix_grads[5],
            state_grad,
            decay_grad,
        )
    )
    returned = (
        return_tails(jnp.concatenate([in_grads[4], in_grads[5], in_grads[6]], axis=1))
        * keep_rows[:, None]
    )
    grad_x = in_grads[0].at[-3:].add(returned[:, :x_width])
    grad_b = in_grads[1].at[-3:].add(returned[:, x_width : x_width + b_width])
    grad_c = in_grads[2].at[-3:].add(returned[:, x_width + b_width :])
    return (
        values,
        grad_x.astype(jnp.bfloat16),
        grad_b.astype(jnp.bfloat16),
        grad_c.astype(jnp.bfloat16),
        mix_grads[4].astype(jnp.bfloat16),
        in_grads[3].astype(jnp.bfloat16),
    )


def shards(
    x_in,
    b_in,
    c_in,
    z_in,
    dt_raw,
    conv_x,
    conv_b,
    conv_c,
    decay_rate,
    dt_bias,
    skip_scale,
    norm_gain,
    w_value,
    resets,
    bucket,
    return_table,
):
    tok_rows = x_in.shape[0]
    gain_weight = norm_gain * w_value
    width_all = HEADS * HEAD_DIM
    tp_index = lax.axis_index("tp")
    tp_count = lax.axis_size("tp")
    moved = (
        lax.all_to_all(x_in, "tp", split_axis=1, concat_axis=0, tiled=True),
        lax.all_to_all(b_in, "tp", split_axis=1, concat_axis=0, tiled=True),
        lax.all_to_all(c_in, "tp", split_axis=1, concat_axis=0, tiled=True),
        lax.all_to_all(z_in, "tp", split_axis=1, concat_axis=0, tiled=True),
        lax.all_to_all(dt_raw, "tp", split_axis=1, concat_axis=0, tiled=True),
    )
    chan_width = x_in.shape[1] // tp_count
    group_width = b_in.shape[1] // tp_count
    head_width = dt_raw.shape[1] // tp_count
    conv_x_part = lax.dynamic_slice_in_dim(conv_x, tp_index * chan_width, chan_width, 1)
    conv_b_part = lax.dynamic_slice_in_dim(conv_b, tp_index * group_width, group_width, 1)
    conv_c_part = lax.dynamic_slice_in_dim(conv_c, tp_index * group_width, group_width, 1)
    rate_part = lax.dynamic_slice_in_dim(decay_rate, tp_index * head_width, head_width, 0)
    bias_part = lax.dynamic_slice_in_dim(dt_bias, tp_index * head_width, head_width, 0)
    skip_part = lax.dynamic_slice_in_dim(skip_scale, tp_index * head_width, head_width, 0)
    gain_part = lax.dynamic_slice_in_dim(gain_weight, tp_index * chan_width, chan_width, 0)

    def send_heads(outgoing):
        return from_behind(outgoing, "ctx", 1)

    def forward_heads(decays, states):
        return carried_in(
            (decays, states), "ctx", link_pairs, pair_identity(decays, states), False
        )[1]

    def backward_heads(decays, grads):
        return carried_in((decays, grads), "ctx", link_pairs, pair_identity(decays, grads), True)[1]

    def return_heads(grads):
        return from_behind(grads, "ctx", -1)

    def value_heads(gated, weight_part):
        squares, numerator = lax.psum(
            (jnp.sum(gated * gated, axis=1), jnp.sum(gated * weight_part[None, :], axis=1)), "tp"
        )
        norm_rms = jnp.sqrt(squares / width_all + epsilon)
        return (numerator / norm_rms, norm_rms)

    results = layer_pass(
        moved[0],
        moved[1],
        moved[2],
        moved[3],
        moved[4],
        resets,
        bucket,
        conv_x_part,
        conv_b_part,
        conv_c_part,
        rate_part,
        bias_part,
        skip_part,
        gain_part,
        return_table,
        send_heads,
        forward_heads,
        backward_heads,
        return_heads,
        value_heads,
    )
    grads = (
        lax.all_to_all(results[1], "tp", split_axis=0, concat_axis=1, tiled=True),
        lax.all_to_all(results[2], "tp", split_axis=0, concat_axis=1, tiled=True),
        lax.all_to_all(results[3], "tp", split_axis=0, concat_axis=1, tiled=True),
        lax.all_to_all(results[4], "tp", split_axis=0, concat_axis=1, tiled=True),
        lax.all_to_all(results[5], "tp", split_axis=0, concat_axis=1, tiled=True),
    )
    values = lax.dynamic_slice_in_dim(results[0], tp_index * tok_rows, tok_rows, 0)
    return (values, grads[0], grads[1], grads[2], grads[3], grads[4])


def solution(mesh):
    in_specs = (
        P(("group", "ctx", "tp"), None),
        P(("group", "ctx", "tp"), None),
        P(("group", "ctx", "tp"), None),
        P(("group", "ctx", "tp"), None),
        P(("group", "ctx", "tp"), None),
        P(),
        P(),
        P(),
        P(),
        P(),
        P(),
        P(),
        P(),
        P(("group", "ctx")),
        P(("group", "ctx")),
        P(),
    )
    out_specs = (
        P(("group", "ctx", "tp")),
        P(("group", "ctx", "tp"), None),
        P(("group", "ctx", "tp"), None),
        P(("group", "ctx", "tp"), None),
        P(("group", "ctx", "tp"), None),
        P(("group", "ctx", "tp"), None),
    )
    return jax.shard_map(shards, mesh=mesh, in_specs=in_specs, out_specs=out_specs, check_vma=False)
```

profile of v0, /device:TPU:0, one launch (start us, length us, event | category | flops | bytes accessed | tf_op | source)
XLA Modules:
  0.0 625.2 jit_solution(7080175646987279698)
XLA Ops:
  27.0 4.9 collective-permute-start
  49.0 37.6 %while.145 = (s32[]{:T(128)}, f32[32,64,128]{2,1,0:T(8,128)}, f32[2,32,64,128]{3,2,1,0:T(8,128)}, f32[2,32]{1,0:T(2,128)}, f32[2,128,32]{1,2,0:T(8,128)}, /*inde...) while((s32[]{:T(128)}, f32[32,64,128]{2,1,0:T(8,128)}, ...), condition=%wide.region_3.4_spmd.clone, body=%wide.region_0.3_spmd.clone.sunk | while | flops 404803776 | bytes 20362988 | solution.py:153
  75.7 4.3 convolution_add_fusion.2
  99.0 19.0 %all-gather.2 = f32[8,1,32]{2,1,0:T(1,128)S(1)} all-gather(f32[1,1,32]{2,1,0:T(1,128)S(1)} %multiply_bitcast_fusion), channel_id=1, replica_groups=mesh['group'=2,'ctx'=8,'tp'=2] {'ctx'}, dimensions={0}, use_global_device_ids=true | all-gather | bytes 1152 | tf_op jit(solution)/shard_map/all_gather | solution.py:28
  118.0 94.2 %all-gather.6.cloned.1.call-done = f32[256,64,128]{2,1,0:T(8,128)} async-done(((f32[32,64,128]{2,1,0:T(8,128)}), f32[256,64,128]{2,1,0:T(8,128)}) %all-gather.6.cloned.1.call-update) | async-done | bytes 8388624 | tf_op jit(solution)/shard_map/all_gather | solution.py:28
  215.9 41.3 %while.146 = (s32[]{:T(128)}, f32[32]{0:T(128)S(1)}, f32[2,128,2048]{2,1,0:T(8,128)}, f32[2,32,1,1]{1,3,2,0:T(1,128)S(1)}, f32[2,128,32]{1,2,0:T(8,128)S(1)}, /*...) while((s32[]{:T(128)}, f32[32]{0:T(128)S(1)}, ...), condition=%wide.region_9.10_spmd.clone, body=%wide.region_6.9_spmd.clone.sunk | while | flops 860430592 | bytes 28045576 | solution.py:197
  217.9 5.4 fusion.262
  226.0 4.2 fusion.266
  238.6 5.4 fusion.262
  246.6 4.2 fusion.266
  257.9 5.2 multiply_reduce_fusion.1
  266.1 6.1 fusion.91
  277.5 115.5 %while.147 = (s32[]{:T(128)}, f32[32,64,128]{2,1,0:T(8,128)}, f32[32]{0:T(128)S(1)}, f32[2,128,2048]{2,1,0:T(8,128)}, f32[2,128,256]{2,1,0:T(8,128)}, /*index=5*...) while((s32[]{:T(128)}, f32[32,64,128]{2,1,0:T(8,128)}, ...), condition=%wide.region_23.24_spmd.clone, body=%wide.region_14.23_spmd.clone.sunk | while | flops 2180289024 | bytes 98383896 | solution.py:197
  297.0 4.2 fusion.288
  301.7 7.2 %fusion.287 = (f32[32,128]{1,0:T(8,128)S(1)}, f32[32,128]{1,0:T(8,128)S(1)}, f32[32,128]{1,0:T(8,128)}, f32[32,128,128]{2,1,0:T(8,128)}, f32[32,128,128]{2,1,0:T(8,128)}) fusion(f32[32,128]{1,0:T(8,128)S(1)} %bitcast.695, f32[32,128]{1,0:T(8,128)S(1)} %bitcast.710, f32[2,128,128]{2,1,0:T(8,128)S(1)} %fusion.285, pred[128,128]{1,0:T(8,128)(4,1)S(1)} %fusion.286, ...), kind=kOutput, calls=%fused_computation.73.clone.1 | convolution fusion | flops 412078080 | bytes 6520832 | tf_op jit(solution)/shard_map/transpose(jvp())/while/body/eval_jaxpr/checkpoint/hts,shp->thp/dot_general | solution.py:99
  319.1 4.1 bitcast_reduce_fusion.8
  327.2 4.6 fusion.292
  348.1 4.2 fusion.288
  352.8 7.2 %fusion.287 = (f32[32,128]{1,0:T(8,128)S(1)}, f32[32,128]{1,0:T(8,128)S(1)}, f32[32,128]{1,0:T(8,128)}, f32[32,128,128]{2,1,0:T(8,128)}, f32[32,128,128]{2,1,0:T(8,128)}) fusion(f32[32,128]{1,0:T(8,128)S(1)} %bitcast.695, f32[32,128]{1,0:T(8,128)S(1)} %bitcast.710, f32[2,128,128]{2,1,0:T(8,128)S(1)} %fusion.285, pred[128,128]{1,0:T(8,128)(4,1)S(1)} %fusion.286, ...), kind=kOutput, calls=%fused_computation.73.clone.1 | convolution fusion | flops 412078080 | bytes 6520832 | tf_op jit(solution)/shard_map/transpose(jvp())/while/body/eval_jaxpr/checkpoint/hts,shp->thp/dot_general | solution.py:99
  370.2 4.1 bitcast_reduce_fusion.8
  378.3 4.6 fusion.292
  386.5 4.6 multiply_reduce_fusion.5
  392.9 5.7 all_to_all.175
  401.2 125.4 %all-gather.8.cloned.1.call-done = f32[256,64,128]{2,1,0:T(8,128)} async-done(((f32[32,64,128]{2,1,0:T(8,128)}), f32[256,64,128]{2,1,0:T(8,128)}) %all-gather.8.cloned.1.call-update) | async-done | bytes 8388624 | tf_op jit(solution)/shard_map/all_gather | solution.py:28
  526.7 15.1 %while.143 = (s32[]{:T(128)}, f32[32,64,128]{2,1,0:T(8,128)S(1)}, s32[]{:T(128)}, f32[8,32]{1,0:T(8,128)}, f32[8,32,64,128]{3,2,1,0:T(8,128)}, /*index=5*/s32[]{:T(128)}, s32[]{:T(128)}, s32[]{:T(128)}, s32[]{:T(128)}) while((s32[]{:T(128)}, f32[32,64,128]{2,1,0:T(8,128)S(1)}, s32[]{:T(128)}, f32[8,32]{1,0:T(8,128)}, ...), condition=%wide.region_25.26_spmd, body=%wide.region_24.25_spmd.sunk | while | flops 524294 | bytes 3146259 | solution.py:37
  545.5 41.5 %while.144 = (s32[]{:T(128)}, f32[32,64,128]{2,1,0:T(8,128)S(1)}, f32[2,128,2048]{2,1,0:T(8,128)}, f32[2,128,256]{2,1,0:T(8,128)}, f32[2,128,32]{1,2,0:T(8,128)}...) while((s32[]{:T(128)}, f32[32,64,128]{2,1,0:T(8,128)S(1)}, ...), condition=%wide.region_33.34_spmd, body=%wide.region_27.33_spmd.sunk | while | flops 808194176 | bytes 27531108 | solution.py:153
  545.5 6.1 fusion.247
  551.6 4.9 bitcast_reduce_fusion.6
  566.2 6.0 fusion.247
  572.3 4.9 bitcast_reduce_fusion.6
  587.0 4.7 multiply_multiply_fusion.3
  610.8 4.6 all_to_all.179
  (684 shorter events, 231.4 us)
Async XLA Ops:
  7.2 89.7 %copy-start = (f32[256]{0:T(256)S(1)}, f32[256]{0:T(256)}, u32[]{:S(2)}) copy-start(f32[256]{0:T(256)} %param.49) | copy-start | bytes 3076
  7.2 8.6 %copy-start.43 = (bf16[128,512]{1,0:T(8,128)(2,1)S(1)}, bf16[128,512]{1,0:T(8,128)(2,1)}, u32[]{:S(2)}) copy-start(bf16[128,512]{1,0:T(8,128)(2,1)} %param.35) | copy-start | bytes 393220
  9.5 11.0 %copy-start.44 = (bf16[128,512]{1,0:T(8,128)(2,1)S(1)}, bf16[128,512]{1,0:T(8,128)(2,1)}, u32[]{:S(2)}) copy-start(bf16[128,512]{1,0:T(8,128)(2,1)} %param.36) | copy-start | bytes 393220
  9.5 7.0 %all-to-all-start.1 = ((bf16[128,2,2048]{0,2,1:T(8,128)(2,1)}), bf16[128,2,2048]{0,2,1:T(8,128)(2,1)S(1)}, u32[]{:S(2)}, u32[]{:S(2)}) async-start(bf16[128,2,2048]{0,2,1:T(8,128)(2,1)} %bitcast.30), calls=%async_computation.1 | async-start | bytes 2097152 | tf_op jit(solution)/shard_map/all_to_all | solution.py:349
  16.6 4.8 all-to-all-start.2
  21.4 4.8 all-to-all-start.3
  24.8 11.5 %copy-start.65 = (f32[4,4096]{1,0:T(4,128)S(1)}, f32[4,4096]{1,0:T(4,128)}, u32[]{:S(2)}) copy-start(f32[4,4096]{1,0:T(4,128)} %param.39) | copy-start | bytes 196612
  24.8 11.6 %copy-start.98 = (f32[4,512]{1,0:T(4,128)S(1)}, f32[4,512]{1,0:T(4,128)}, u32[]{:S(2)}) copy-start(f32[4,512]{1,0:T(4,128)} %param.40) | copy-start | bytes 24580
  24.8 11.7 %copy-start.109 = (f32[64]{0:T(128)S(1)}, f32[64]{0:T(128)}, u32[]{:S(2)}) copy-start(f32[64]{0:T(128)} %param.43) | copy-start | bytes 772
  24.9 11.9 %copy-start.110 = (f32[64]{0:T(128)S(1)}, f32[64]{0:T(128)}, u32[]{:S(2)}) copy-start(f32[64]{0:T(128)} %param.42) | copy-start | bytes 772
  26.3 8.9 %copy-start.34 = (bf16[2,128,256]{2,1,0:T(8,128)(2,1)}, bf16[2,128,256]{2,1,0:T(8,128)(2,1)S(1)}, u32[]{:S(2)}) copy-start(bf16[2,128,256]{2,1,0:T(8,128)(2,1)S(1)} %copy.245) | copy-start | bytes 393220
  27.0 10.4 %collective-permute-start = (bf16[3,2560]{1,0:T(4,128)(2,1)S(1)}, bf16[3,2560]{1,0:T(4,128)(2,1)S(1)}, u32[]{:S(2)}, u32[]{:S(2)}) collective-permute-start(bf16[3,2560]{1,0:T(4,128)(2,1)S(1)} %maximum_multiply_fusion), channel_id=1, source_target_pairs={{0,2},{2,4},{4,6},{6,8},{8,10},{10,12},{12,14},{1,3},{3,5},{5,7},{... | collective-permute-start | bytes 46088 | tf_op jit(solution)/shard_map/ppermute | solution.py:21
  31.9 4.8 all-to-all-start
  35.2 177.0 %all-gather.6.cloned.1.call-start = ((), (), s32[]{:S(2)}) async-start(), calls=%async_computation.10 | async-start | bytes 9437184 | tf_op jit(solution)/shard_map/all_gather | solution.py:28
  36.5 6.7 %copy-start.67 = (f32[1,256]{1,0:T(1,128)}, f32[1,256]{1,0:T(1,128)S(1)}, u32[]{:S(2)}) copy-start(f32[1,256]{1,0:T(1,128)S(1)} %get-tuple-element.2292) | copy-start | bytes 3076
  36.5 6.7 %copy-start.69 = (f32[1,256]{1,0:T(1,128)}, f32[1,256]{1,0:T(1,128)S(1)}, u32[]{:S(2)}) copy-start(f32[1,256]{1,0:T(1,128)S(1)} %get-tuple-element.2293) | copy-start | bytes 3076
  36.5 6.7 %copy-start.71 = (f32[1,256]{1,0:T(1,128)}, f32[1,256]{1,0:T(1,128)S(1)}, u32[]{:S(2)}) copy-start(f32[1,256]{1,0:T(1,128)S(1)} %get-tuple-element.2294) | copy-start | bytes 3076
  36.5 6.7 %copy-start.73 = (f32[1,256]{1,0:T(1,128)}, f32[1,256]{1,0:T(1,128)S(1)}, u32[]{:S(2)}) copy-start(f32[1,256]{1,0:T(1,128)S(1)} %get-tuple-element.2295) | copy-start | bytes 3076
  36.7 6.6 %copy-start.55 = (f32[256]{0:T(256)}, f32[256]{0:T(256)S(1)}, u32[]{:S(2)}) copy-start(f32[256]{0:T(256)S(1)} %get-tuple-element.2305) | copy-start | bytes 3076
  36.7 6.6 %copy-start.58 = (f32[256]{0:T(256)}, f32[256]{0:T(256)S(1)}, u32[]{:S(2)}) copy-start(f32[256]{0:T(256)S(1)} %get-tuple-element.2304) | copy-start | bytes 3076
  36.7 6.6 %copy-start.61 = (f32[256]{0:T(256)}, f32[256]{0:T(256)S(1)}, u32[]{:S(2)}) copy-start(f32[256]{0:T(256)S(1)} %get-tuple-element.2312) | copy-start | bytes 3076
  60.1 6.6 %copy-start.32 = (f32[2,128,32]{2,1,0:T(8,128)}, f32[2,128,32]{2,1,0:T(8,128)S(1)}, u32[]{:S(2)}) copy-start(f32[2,128,32]{2,1,0:T(8,128)S(1)} %get-tuple-element.3013) | copy-start | bytes 98308 | tf_op jit(solution)/shard_map/jvp()/while
  89.0 5.7 all-to-all-start.4
  92.6 434.0 %all-gather.8.cloned.1.call-start = ((), (), s32[]{:S(2)}) async-start(), calls=%async_computation.11 | async-start | bytes 9437184 | tf_op jit(solution)/shard_map/all_gather | solution.py:28
  96.9 115.4 %copy-start.75 = (f32[1,256]{1,0:T(1,128)}, f32[1,256]{1,0:T(1,128)S(1)}, u32[]{:S(2)}) copy-start(f32[1,256]{1,0:T(1,128)S(1)} %get-tuple-element.2296) | copy-start | bytes 3076
  257.9 7.6 %copy-start.104 = (f32[1,256]{1,0:T(1,128)S(1)}, f32[1,256]{1,0:T(1,128)}, u32[]{:S(2)}) copy-start(f32[1,256]{1,0:T(1,128)} %fusion.127) | copy-start | bytes 3076
  257.9 8.3 %copy-start.6 = (f32[256,2048]{1,0:T(8,128)S(1)}, f32[256,2048]{1,0:T(8,128)}, u32[]{:S(2)}) copy-start(f32[256,2048]{1,0:T(8,128)} %copy-done.5) | copy-start | bytes 6291460
  289.2 20.8 %copy-start.53 = (f32[32]{0:T(128)}, f32[32]{0:T(128)S(1)}, u32[]{:S(2)}) copy-start(f32[32]{0:T(128)S(1)} %get-tuple-element.3157) | copy-start | bytes 388 | tf_op jit(solution)/shard_map/transpose(jvp())/while
  340.3 20.8 %copy-start.53 = (f32[32]{0:T(128)}, f32[32]{0:T(128)S(1)}, u32[]{:S(2)}) copy-start(f32[32]{0:T(128)S(1)} %get-tuple-element.3157) | copy-start | bytes 388 | tf_op jit(solution)/shard_map/transpose(jvp())/while
  545.4 41.5 %copy-start.46 = (f32[1,2048]{1,0:T(1,128)S(1)}, f32[1,2048]{1,0:T(1,128)}, u32[]{:S(2)}) copy-start(f32[1,2048]{1,0:T(1,128)} %copy-done.45) | copy-start | bytes 24580
  545.4 41.5 %copy-start.57 = (f32[256]{0:T(256)S(1)}, f32[256]{0:T(256)}, u32[]{:S(2)}) copy-start(f32[256]{0:T(256)} %copy-done.55) | copy-start | bytes 3076
  594.4 6.5 %collective-permute-start.1 = (f32[3,2560]{1,0:T(4,128)S(1)}, f32[3,2560]{1,0:T(4,128)S(1)}, u32[]{:S(2)}, u32[]{:S(2)}) collective-permute-start(f32[3,2560]{1,0:T(4,128)S(1)} %pad_maximum_fusion.3), channel_id=1, source_target_pairs={{2,0},{4,2},{6,4},{8,6},{10,8},{12,10},{14,12},{3,1},{5,3},{7,5},{... | collective-permute-start | bytes 92168 | tf_op jit(solution)/shard_map/ppermute | solution.py:21
  (123 other events, 320.7 us)
Sparse Core Ops, SparseCore 0:
  86.8 125.3 all-gather.5
  393.1 133.4 all-gather.7
where the time goes:
time: 636 us; the launch traced here: 625 us
  waiting for transfers between devices  223 us (35%)
  local copies, waits for them, and re-layouts  124 us (19%)
  matrix products  100 us (16%)
  other arithmetic  77.5 us (12%)
  blocking collectives  43.1 us (7%)
  starting transfers between devices  23.5 us (4%)
  between operations  17.7 us (3%)
  loops' own time  16.6 us (3%)
    all_gather x2, waiting for transfers between devices, carried_in(): gathered = jax.tree.map(lambda a: lax.all_gather(a, axis), part)  220 us
    dot_general x8, matrix products, block_output(): jnp.einsum('thn,hpn->thp', c_heads, start_state, precision=highest)  35.3 us
    dot_general x6, matrix products, block_output(): jnp.einsum('hts,shp->thp', mixing, x_conv.reshape(row_count, head_count,...  32 us
    dot_general x6, matrix products, block_state(): state_add = jnp.einsum('shp,shn->hpn', x_heads, b_heads, precision=highest)  29.1 us
    all_gather x1, blocking collectives, carried_in(): gathered = jax.tree.map(lambda a: lax.all_gather(a, axis), part)  19 us
    unnamed x181, local copies, waits for them, and re-layouts  18 us
    dynamic_update_slice x40, local copies, waits for them, and re-layouts, local_states(): end_state, (starts, decays) = lax.scan(advance, initial, pieces)  16.9 us
    another operation x32, local copies, waits for them, and re-layouts  15.9 us
  transfers between devices with their start and end apart: 9, of which 5 were waited for; matrix products, arithmetic and copies ran while one was open for 2% of the time, Pallas kernels for 0%

commit v1 on v0

v1 whole, which is shorter than its diff:
```python
import jax
import jax.numpy as jnp
from jax import lax
from jax.experimental import pallas as pl
from jax.experimental.pallas import tpu as pltpu
from jax.sharding import PartitionSpec as P

HEADS = 64
HEAD_DIM = 64
GROUPS = 4
STATE = 128
PAIR = 2 * HEAD_DIM
PAIRS_PER_GROUP = HEADS // GROUPS // 2

epsilon = 1e-05
highest = lax.Precision.HIGHEST
f32 = jnp.float32
bf16 = jnp.bfloat16


def dot(a, b, ca, cb):
    return lax.dot_general(a, b, (((ca,), (cb,)), ((), ())), preferred_element_type=f32)


def sigmoid(u):
    return 1.0 / (1.0 + jnp.exp(-u))


def conv_pre(ext, x_ref, tail_ref, w_ref, valid):
    rows = x_ref.shape[0]
    ext[0:8, :] = tail_ref[...]
    ext[8 : 8 + rows, :] = x_ref[...].astype(f32)
    total = w_ref[0:1, :] * ext[8 : 8 + rows, :]
    for k in range(1, 4):
        total = total + w_ref[k : k + 1, :] * ext[8 - k : 8 - k + rows, :] * valid[:, k - 1 : k]
    return total


def conv_back(ext, du, w_ref, valid):
    rows = du.shape[0]
    ext[...] = jnp.zeros(ext.shape, f32)
    grad = w_ref[0:1, :] * du
    head = jnp.zeros((8, du.shape[1]), f32)
    for k in range(1, 4):
        ext[8 : 8 + rows, :] = w_ref[k : k + 1, :] * du * valid[:, k - 1 : k]
        grad = grad + ext[8 + k : 8 + k + rows, :]
        head = head + ext[k : k + 8, :]
    return grad, head


def silu_back(grad, u):
    s = sigmoid(u)
    return grad * (s * (1.0 + u * (1.0 - s)))


def spread(cols, i):
    rows = cols.shape[0]
    lane = lax.broadcasted_iota(jnp.int32, (rows, PAIR), 1)
    return jnp.where(lane < HEAD_DIM, cols[:, i : i + 1], cols[:, i + 1 : i + 2])


def pair_put(*cols):
    rows = cols[0].shape[0]
    lane = lax.broadcasted_iota(jnp.int32, (rows, 8), 1)
    out = jnp.zeros((rows, 8), f32)
    for i, c in enumerate(cols):
        out = jnp.where(lane == i, c, out)
    return out


def conv_kernel(
    x, b, c, tx, tb, tc, wx, wb, wc, valid_ref, cols_ref,
    xc, bc, cc, ux, ub, uc, add, ext,
):
    k = pl.program_id(0)
    valid = valid_ref[...]

    @pl.when(lax.rem(k, PAIRS_PER_GROUP) == 0)
    def _():
        u = conv_pre(ext, b, tb, wb, valid)
        ub[...] = u
        bc[...] = (u * sigmoid(u)).astype(bf16)
        u = conv_pre(ext, c, tc, wc, valid)
        uc[...] = u
        cc[...] = (u * sigmoid(u)).astype(bf16)

    u = conv_pre(ext, x, tx, wx, valid)
    ux[...] = u
    narrow = (u * sigmoid(u)).astype(bf16)
    xc[...] = narrow
    cols = cols_ref[0]
    weighted = (narrow.astype(f32) * spread(cols, 4)).astype(bf16)
    add[...] = dot(weighted, bc[...], 0, 0).astype(bf16)


def fade(cols, rowvals, seg, j):
    gap = cols[:, j : j + 1] - rowvals[j : j + 1, :]
    return jnp.exp(jnp.minimum(gap, 0.0) + seg)


def mix_kernel(
    xc, bc, cc, z, state, cols_ref, rows_ref, seg_ref, gw, skip,
    mixed, squares, numer, scores,
):
    k = pl.program_id(0)

    @pl.when(lax.rem(k, PAIRS_PER_GROUP) == 0)
    def _():
        scores[...] = dot(cc[...], bc[...], 1, 1)

    @pl.when(k == 0)
    def _():
        squares[...] = jnp.zeros(squares.shape, f32)
        numer[...] = jnp.zeros(numer.shape, f32)

    cols = cols_ref[0]
    rowvals = rows_ref[0]
    x = xc[...]
    parts = []
    for j in range(2):
        m = scores[...] * fade(cols, rowvals, seg_ref[...], j) * rowvals[2 + j : 3 + j, :]
        parts.append(dot(m.astype(bf16), x[:, j * HEAD_DIM : (j + 1) * HEAD_DIM], 1, 0))
    within = jnp.concatenate(parts, axis=1)
    carried = dot(cc[...], state[...], 1, 1) * spread(cols, 2)
    m = within + carried + skip[...] * x.astype(f32)
    mixed[...] = m
    zz = z[...].astype(f32)
    gated = m * (zz * sigmoid(zz))
    squares[...] += gated * gated
    numer[...] += gated * gw[...]


def back_kernel(
    xc, bc, cc, z, state, cols_ref, rows_ref, seg_ref, gw, skip, mixed, vcols,
    dz, dx, dcg, dbg, ds, colout, rowout, scores, dscores, dcacc,
):
    k = pl.program_id(0)
    place = lax.rem(k, PAIRS_PER_GROUP)

    @pl.when(place == 0)
    def _():
        scores[...] = dot(cc[...], bc[...], 1, 1)
        dscores[...] = jnp.zeros(dscores.shape, f32)
        dcacc[...] = jnp.zeros(dcacc.shape, f32)

    cols = cols_ref[0]
    rowvals = rows_ref[0]
    x = xc[...]
    zz = z[...].astype(f32)
    m = mixed[...]
    s = sigmoid(zz)
    gate = zz * s
    gated = m * gate
    dgated = vcols[:, 0:1] * (gw[...] - vcols[:, 1:2] * gated)
    dz[...] = (dgated * m * (s * (1.0 + zz * (1.0 - s)))).astype(bf16)
    dy = dgated * gate
    dyb = dy.astype(bf16)
    outs = []
    rowsums = []
    colsums = []
    for j in range(2):
        sl = slice(j * HEAD_DIM, (j + 1) * HEAD_DIM)
        dt_row = rowvals[2 + j : 3 + j, :]
        f = fade(cols, rowvals, seg_ref[...], j)
        fd = f * dt_row
        sc = scores[...]
        dm = dot(dyb[:, sl], x[:, sl], 1, 1)
        outs.append(dot((sc * fd).astype(bf16), dyb[:, sl], 0, 0))
        dscores[...] += fd * dm
        q = sc * f * dm
        rowsums.append(jnp.sum(q * dt_row, axis=1, keepdims=True))
        colsums.append(jnp.sum(q, axis=0, keepdims=True))
    dx[...] = jnp.concatenate(outs, axis=1) + skip[...] * dy
    reach = dy * spread(cols, 2)
    reachb = reach.astype(bf16)
    carried = dot(cc[...], state[...], 1, 1)
    both = reach * carried
    for j in range(2):
        sl = slice(j * HEAD_DIM, (j + 1) * HEAD_DIM)
        rowsums[j] = rowsums[j] + jnp.sum(both[:, sl], axis=1, keepdims=True)
    dcacc[...] += dot(reachb, state[...], 1, 0)
    ds[...] = dot(reachb, cc[...], 0, 0).astype(bf16)
    colout[0] = pair_put(*rowsums)
    sub = lax.broadcasted_iota(jnp.int32, (8, colsums[0].shape[1]), 0)
    rowout[0] = jnp.where(sub == 0, colsums[0], jnp.where(sub == 1, colsums[1], 0.0))

    @pl.when(place == PAIRS_PER_GROUP - 1)
    def _():
        d = dscores[...].astype(bf16)
        dcg[...] = dcacc[...] + dot(d, bc[...], 1, 0)
        dbg[...] = dot(d, cc[...], 0, 0)


def last_kernel(
    xc, bc, gstate, state, cols_ref, dx, dcg, dbg, ux, ub, uc, wx, wb, wc, valid_ref,
    gx, gb, gc, hx, hb, hc, lx, lb, lc, stats, inner, dbacc, ext,
):
    k = pl.program_id(0)
    place = lax.rem(k, PAIRS_PER_GROUP)
    valid = valid_ref[...]
    rows = xc.shape[0]

    def finish(grad, u, w, out, head, last):
        g, h = conv_back(ext, silu_back(grad, u[...]), w, valid)
        out[...] = g.astype(bf16)
        head[...] = h
        last[...] = g[rows - 8 :, :]

    @pl.when(place == 0)
    def _():
        dbacc[...] = dbg[...]
        finish(dcg[...], uc, wc, gc, hc, lc)

    cols = cols_ref[0]
    x = xc[...].astype(f32)
    we = spread(cols, 4)
    g = gstate[...]
    gbx = dot(bc[...], g, 1, 1)
    xg = x * gbx
    stats[0] = pair_put(
        jnp.sum(xg[:, :HEAD_DIM], axis=1, keepdims=True),
        jnp.sum(xg[:, HEAD_DIM:], axis=1, keepdims=True),
    )
    gs = g.astype(f32) * state[...].astype(f32)
    sub = lax.broadcasted_iota(jnp.int32, (8, STATE), 0)
    inner[...] = jnp.where(
        sub == 0,
        jnp.sum(gs[:HEAD_DIM], axis=0, keepdims=True),
        jnp.where(sub == 1, jnp.sum(gs[HEAD_DIM:], axis=0, keepdims=True), 0.0),
    )[None]
    dbacc[...] += dot((x * we).astype(bf16), g, 1, 0)
    finish(dx[...] + we * gbx, ux, wx, gx, hx, lx)

    @pl.when(place == PAIRS_PER_GROUP - 1)
    def _():
        finish(dbacc[...], ub, wb, gb, hb, lb)


def shift_rows(values, amount):
    filler = jnp.zeros((amount,) + values.shape[1:], values.dtype)
    return jnp.concatenate([filler, values[: values.shape[0] - amount]], axis=0)


def hop(value, steps):
    count = lax.axis_size("ctx")
    initial, last = max(0, -steps), min(count, count - steps)
    return lax.ppermute(value, "ctx", [(i, i + steps) for i in range(initial, last)])


def carry(states, decays, sign):
    count = lax.axis_size("ctx")
    me = lax.axis_index("ctx")
    heads = decays.shape[1]
    shape3 = (heads, HEAD_DIM, STATE)
    held = hop(states, sign)
    span = 1
    while span < count - 1:
        prod = jnp.ones((heads,), f32)
        for i in range(1, span + 1):
            prod = prod * lax.dynamic_index_in_dim(
                decays, jnp.clip(me - sign * i, 0, count - 1), 0, False
            )
        got = hop(held, sign * span)
        total = prod[:, None, None] * got.astype(f32).reshape(shape3) + held.astype(f32).reshape(
            shape3
        )
        held = total.reshape(states.shape).astype(bf16)
        span *= 2
    return held


def shards(
    x_in, b_in, c_in, z_in, dt_raw, conv_x, conv_b, conv_c, decay_rate, dt_bias, skip_scale,
    norm_gain, w_value, resets, bucket, return_table,
):
    tok = x_in.shape[0]
    tp = lax.axis_index("tp")
    tpn = lax.axis_size("tp")

    def fwd(a):
        return lax.all_to_all(a, "tp", split_axis=1, concat_axis=0, tiled=True)

    def rev(a):
        return lax.all_to_all(a, "tp", split_axis=0, concat_axis=1, tiled=True)

    dt_in = fwd(dt_raw).astype(f32)
    x, b, c, z = fwd(x_in), fwd(b_in), fwd(c_in), fwd(z_in)
    T = x.shape[0]
    W, N, H = x.shape[1], b.shape[1], dt_in.shape[1]
    pairs = H // 2

    def mine(a, width):
        return lax.dynamic_slice_in_dim(a, tp * width, width, a.ndim - 1)

    wx, wb, wc = mine(conv_x, W), mine(conv_b, N), mine(conv_c, N)
    rate, bias, skip = mine(decay_rate, H), mine(dt_bias, H), mine(skip_scale, H)
    gw = mine(norm_gain * w_value, W)[None, :]
    skip_row = jnp.repeat(skip, HEAD_DIM)[None, :]

    real = resets.astype(f32)
    keep = jnp.stack([1.0 - jnp.maximum(real[-2], real[-1]), 1.0 - real[-1], jnp.ones((), f32)])
    second = jnp.maximum(real, shift_rows(real, 1))
    third = jnp.maximum(second, shift_rows(real, 2))
    valid = 1.0 - jnp.stack([real, second, third] + [real] * 5, axis=1)

    outgoing = jnp.concatenate([x[-3:], b[-3:], c[-3:]], axis=1) * keep.astype(bf16)[:, None]
    incoming = jnp.pad(hop(outgoing, 1).astype(f32), ((5, 0), (0, 0)))
    tx, tb, tc = incoming[:, :W], incoming[:, W : W + N], incoming[:, W + N :]

    dt_pre = dt_in + bias[None, :]
    dt = jax.nn.softplus(dt_pre)
    r_i = lax.broadcasted_iota(jnp.int32, (T, T), 0)
    c_i = lax.broadcasted_iota(jnp.int32, (T, T), 1)
    lower = jnp.where(r_i >= c_i, 1.0, 0.0)
    sums = jnp.dot(
        lower, jnp.concatenate([-dt * rate[None, :], real[:, None]], axis=1), precision=highest
    )
    cum, counts = sums[:, :H], jnp.round(sums[:, H])
    seg = jnp.where((r_i >= c_i) & (counts[:, None] == counts[None, :]), 0.0, -1e30)
    reach = jnp.exp(cum) * jnp.where(counts == 0.0, 1.0, 0.0)[:, None]
    tail_decay = jnp.exp(cum[-1][None, :] - cum) * jnp.where(counts == counts[-1], 1.0, 0.0)[:, None]
    we = tail_decay * dt
    decay = reach[-1]
    decays = lax.all_gather(decay, "ctx")

    def to_pairs(a):
        return a.reshape(T, pairs, 2).transpose(1, 0, 2)

    cols = jnp.concatenate([to_pairs(cum), to_pairs(reach), to_pairs(we), to_pairs(tail_decay)], 2)
    rowvals = jnp.concatenate(
        [cum.T.reshape(pairs, 2, T), dt.T.reshape(pairs, 2, T), jnp.zeros((pairs, 4, T), f32)], 1
    )

    def sds(shape, dtype=f32):
        return jax.ShapeDtypeStruct(shape, dtype)

    per = PAIRS_PER_GROUP
    px = pl.BlockSpec((T, PAIR), lambda k: (0, k))
    pg = pl.BlockSpec((T, STATE), lambda k: (0, k // per))
    t8x = pl.BlockSpec((8, PAIR), lambda k: (0, k))
    t8g = pl.BlockSpec((8, STATE), lambda k: (0, k // per))
    w4x = pl.BlockSpec((4, PAIR), lambda k: (0, k))
    w4g = pl.BlockSpec((4, STATE), lambda k: (0, k // per))
    r1x = pl.BlockSpec((1, PAIR), lambda k: (0, k))
    v8 = pl.BlockSpec((T, 8), lambda k: (0, 0))
    c8 = pl.BlockSpec((1, T, 8), lambda k: (k, 0, 0))
    r8 = pl.BlockSpec((1, 8, T), lambda k: (k, 0, 0))
    st = pl.BlockSpec((PAIR, STATE), lambda k: (k, 0))
    tt = pl.BlockSpec((T, T), lambda k: (0, 0))
    acc = pl.BlockSpec((T, PAIR), lambda k: (0, 0))
    params = pltpu.CompilerParams(
        dimension_semantics=("arbitrary",), vmem_limit_bytes=32 * 1024 * 1024
    )
    ext = pltpu.VMEM((T + 16, PAIR), f32)
    square = pltpu.VMEM((T, T), f32)

    xc, bc, cc, ux, ub, uc, add = pl.pallas_call(
        conv_kernel,
        grid=(pairs,),
        in_specs=[px, pg, pg, t8x, t8g, t8g, w4x, w4g, w4g, v8, c8],
        out_specs=[px, pg, pg, px, pg, pg, st],
        out_shape=[
            sds((T, W), bf16), sds((T, N), bf16), sds((T, N), bf16),
            sds((T, W)), sds((T, N)), sds((T, N)), sds((W, STATE), bf16),
        ],
        scratch_shapes=[ext],
        compiler_params=params,
    )(x, b, c, tx, tb, tc, wx, wb, wc, valid, cols)

    state = carry(add, decays, 1)

    mixed, squares, numer = pl.pallas_call(
        mix_kernel,
        grid=(pairs,),
        in_specs=[px, pg, pg, px, st, c8, r8, tt, r1x, r1x],
        out_specs=[px, acc, acc],
        out_shape=[sds((T, W)), sds((T, PAIR)), sds((T, PAIR))],
        scratch_shapes=[square],
        compiler_params=params,
    )(xc, bc, cc, z, state, cols, rowvals, seg, gw, skip_row)

    both = lax.psum(jnp.stack([jnp.sum(squares, axis=1), jnp.sum(numer, axis=1)]), "tp")
    width_all = W * tpn
    rms = jnp.sqrt(both[0] / width_all + epsilon)
    values = both[1] / rms
    table_n = return_table.shape[0]
    onehot = bucket[:, None] == lax.broadcasted_iota(jnp.int32, (1, table_n), 1)
    target = jnp.sum(jnp.where(onehot, return_table[None, :], 0.0), axis=1)
    vscale = (values - target) / rms
    vcols = jnp.stack([vscale, values / (rms * width_all)] + [vscale] * 6, axis=1)

    dz, dx, dcg, dbg, ds, colout, rowout = pl.pallas_call(
        back_kernel,
        grid=(pairs,),
        in_specs=[px, pg, pg, px, st, c8, r8, tt, r1x, r1x, px, v8],
        out_specs=[px, px, pg, pg, st, c8, r8],
        out_shape=[
            sds((T, W), bf16), sds((T, W)), sds((T, N)), sds((T, N)), sds((W, STATE), bf16),
            sds((pairs, T, 8)), sds((pairs, 8, T)),
        ],
        scratch_shapes=[square, square, pltpu.VMEM((T, STATE), f32)],
        compiler_params=params,
    )(xc, bc, cc, z, state, cols, rowvals, seg, gw, skip_row, mixed, vcols)

    grad_z = rev(dz)
    gstate = carry(ds, decays, -1)

    gx, gb, gc, hx, hb, hc, lx, lb, lc, stats, inner = pl.pallas_call(
        last_kernel,
        grid=(pairs,),
        in_specs=[px, pg, st, st, c8, px, pg, pg, px, pg, pg, w4x, w4g, w4g, v8],
        out_specs=[px, pg, pg, t8x, t8g, t8g, t8x, t8g, t8g, c8, r8s(STATE)],
        out_shape=[
            sds((T, W), bf16), sds((T, N), bf16), sds((T, N), bf16),
            sds((8, W)), sds((8, N)), sds((8, N)), sds((8, W)), sds((8, N)), sds((8, N)),
            sds((pairs, T, 8)), sds((pairs, 8, STATE)),
        ],
        scratch_shapes=[pltpu.VMEM((T, STATE), f32), ext],
        compiler_params=params,
    )(xc, bc, gstate, state, cols, dx, dcg, dbg, ux, ub, uc, wx, wb, wc, valid)

    def from_cols(a):
        return a[:, :, :2].transpose(1, 0, 2).reshape(T, H)

    row_part = from_cols(colout)
    col_sum = rowout[:, :2, :].reshape(H, T).T
    xg = from_cols(stats)
    ginner = jnp.sum(inner[:, :2, :], axis=2).reshape(H)
    tail_part = we * xg
    dcum = row_part - dt * col_sum - tail_part
    at_end = jnp.sum(tail_part, axis=0) + decay * ginner
    rev_sum = jnp.dot(lower.T, dcum, precision=highest) + at_end[None, :]
    ddt = col_sum + tail_decay * xg - rate[None, :] * rev_sum
    grad_dt = rev((ddt * jax.nn.sigmoid(dt_pre)).astype(bf16))

    heads3 = jnp.concatenate([hx, hb, hc], axis=1)[5:8]
    last3 = jnp.concatenate([lx, lb, lc], axis=1)[5:8]
    fixed = (last3 + hop(heads3, -1) * keep[:, None]).astype(bf16)
    gx = lax.dynamic_update_slice(gx, fixed[:, :W], (T - 3, 0))
    gb = lax.dynamic_update_slice(gb, fixed[:, W : W + N], (T - 3, 0))
    gc = lax.dynamic_update_slice(gc, fixed[:, W + N :], (T - 3, 0))
    out_values = lax.dynamic_slice_in_dim(values, tp * tok, tok, 0)
    return (out_values, rev(gx), rev(gb), rev(gc), grad_z, grad_dt)


def r8s(width):
    return pl.BlockSpec((1, 8, width), lambda k: (k, 0, 0))


def solution(mesh):
    row = P(("group", "ctx", "tp"), None)
    seq = P(("group", "ctx"))
    return jax.shard_map(
        shards,
        mesh=mesh,
        in_specs=(row,) * 5 + (P(),) * 8 + (seq, seq, P()),
        out_specs=(P(("group", "ctx", "tp")),) + (row,) * 5,
        check_vma=False,
    )
```

time: 636 us -> 340 us (0.53); the launches traced: 625 us -> 336 us
  waiting for transfers between devices: 223 us -> 83.9 us
  matrix products: 100 us -> 0.85 us
  Pallas kernels: 0 us -> 62.6 us
  local copies, waits for them, and re-layouts: 124 us -> 70.1 us
  other arithmetic: 77.5 us -> 25.1 us
  starting transfers between devices: 23.5 us -> 43.3 us
  loops' own time: 16.6 us -> 0 us
  between operations: 17.7 us -> 3.4 us
    all_gather x2 -> x0, waiting for transfers between devices: 220 us -> none  [carried_in(): gathered = jax.tree.map(lambda a: lax.all_gather(a, axis), part)]
    dot_general x29 -> x2, matrix products: 100 us -> 0.85 us  [the longest x1 0.48 us: shards(): rev_sum = jnp.dot(lower.T, dcum, precision=highest) + at_end[None, :]]
    ppermute x2 -> x10, waiting for transfers between devices: 0.01 us -> 79 us  [hop(): lax.ppermute(value, 'ctx', [(i, i + steps) for i in range(initial, last)])]
    pallas_call x0 -> x4, Pallas kernels: none -> 62.6 us  [the longest x1 29 us: shards(): pl.pallas_call(back_kernel, grid=(pairs,), in_specs=[px, pg, pg, px, st,...]
    dynamic_update_slice x66 -> x3, local copies, waits for them, and re-layouts: 30.7 us -> 0.34 us  [the longest x1 0.22 us: shards(): gx = lax.dynamic_update_slice(gx, fixed[:, :W], (T - 3, 0))]
    unnamed x181 -> x153, local copies, waits for them, and re-layouts: 18 us -> 39.5 us
    ppermute x2 -> x10, starting transfers between devices: 6.15 us -> 26 us  [hop(): lax.ppermute(value, 'ctx', [(i, i + steps) for i in range(initial, last)])]
    another operation x6 -> x0, loops' own time: 16.6 us -> none  [the longest x2 14.3 us: local_mix(): _, outputs = lax.scan(advance, jnp.ones((head_count,), jnp.float32), pieces)]
  transfers between devices with their start and end apart: 9 -> 15, of which waited for: 5 -> 9; matrix products, arithmetic and copies ran while one was open for 2% -> 11% of each run, Pallas kernels for 0% -> 0%
where the time goes in v1:
time: 340 us; the launch traced here: 336 us
  waiting for transfers between devices  83.9 us (25%)
  local copies, waits for them, and re-layouts  70.1 us (21%)
  Pallas kernels  62.6 us (18%)
  blocking collectives  47.2 us (14%)
  starting transfers between devices  43.3 us (13%)
  other arithmetic  25.1 us (7%)
  between operations  3.4 us (1%)
    ppermute x10, waiting for transfers between devices, hop(): lax.ppermute(value, 'ctx', [(i, i + steps) for i in range(initial, last)])  79 us
    unnamed x153, local copies, waits for them, and re-layouts  39.5 us
    pallas_call x1, Pallas kernels, shards(): pl.pallas_call(back_kernel, grid=(pairs,), in_specs=[px, pg, pg, px, st,...  29 us
    ppermute x10, starting transfers between devices, hop(): lax.ppermute(value, 'ctx', [(i, i + steps) for i in range(initial, last)])  26 us
    all_gather x1, blocking collectives, shards(): decays = lax.all_gather(decay, 'ctx')  24 us
    all_to_all x5, blocking collectives, rev(): return lax.all_to_all(a, 'tp', split_axis=0, concat_axis=1, tiled=True)  20.7 us
    all_to_all x5, starting transfers between devices, fwd(): return lax.all_to_all(a, 'tp', split_axis=1, concat_axis=0, tiled=True)  17.3 us
    pallas_call x1, Pallas kernels, shards(): pl.pallas_call(last_kernel, grid=(pairs,), in_specs=[px, pg, st, st, c8,...  15 us
  transfers between devices with their start and end apart: 15, of which 9 were waited for; matrix products, arithmetic and copies ran while one was open for 11% of the time, Pallas kernels for 0%

profile of v1, /device:TPU:0, one launch (start us, length us, event | category | flops | bytes accessed | tf_op | source)
XLA Modules:
  0.0 336.3 jit_solution(934778525955473648)
XLA Ops:
  2.3 3.4 %all-to-all-start.2 = ((bf16[128,2,256]{2,0,1:T(8,128)(2,1)}), bf16[128,2,256]{2,0,1:T(8,128)(2,1)S(1)}, u32[]{:S(2)}, u32[]{:S(2)}) async-start(bf16[128,2,256]{2,0,1:T(8,128)(2,1)} %bitcast.155), calls=%async_computation.2 | async-start | bytes 262144 | tf_op jit(solution)/shard_map/all_to_all | solution.py:281
  8.7 3.4 %all-to-all-start.1 = ((bf16[128,2,256]{2,0,1:T(8,128)(2,1)}), bf16[128,2,256]{2,0,1:T(8,128)(2,1)S(1)}, u32[]{:S(2)}, u32[]{:S(2)}) async-start(bf16[128,2,256]{2,0,1:T(8,128)(2,1)} %bitcast.156), calls=%async_computation.1 | async-start | bytes 262144 | tf_op jit(solution)/shard_map/all_to_all | solution.py:281
  13.5 3.6 %all-to-all-start = ((bf16[128,2,2048]{2,0,1:T(8,128)(2,1)}), bf16[128,2,2048]{2,0,1:T(8,128)(2,1)S(1)}, u32[]{:S(2)}, u32[]{:S(2)}) async-start(bf16[128,2,2048]{2,0,1:T(8,128)(2,1)} %bitcast.154), calls=%async_computation | async-start | bytes 2097152 | tf_op jit(solution)/shard_map/all_to_all | solution.py:281
  23.1 5.5 %collective-permute-start = (bf16[3,2560]{1,0:T(4,128)(2,1)}, bf16[3,2560]{1,0:T(4,128)(2,1)}, u32[]{:S(2)}, u32[]{:S(2)}) collective-permute-start(bf16[3,2560]{1,0:T(4,128)(2,1)} %maximum_multiply_fusion), channel_id=1, source_target_pairs={{0,2},{2,4},{4,6},{6,8},{8,10},{10,12},{12,14},{1,3},{3,5},{5,7},{... | collective-permute-start | bytes 46088 | tf_op jit(solution)/shard_map/ppermute | solution.py:247
  28.5 3.2 all-to-all-start.3
  42.0 9.8 %shard_map.199 = (bf16[256,2048]{1,0:T(8,128)(2,1)S(1)}, bf16[256,256]{1,0:T(8,128)(2,1)S(1)}, bf16[256,256]{1,0:T(8,128)(2,1)S(1)}, f32[256,2048]{1,0:T(8,128)S...) custom-call(bf16[256,2048]{1,0:T(8,128)(2,1)S(1)} %bitcast.162, ...), custom_call_target="tpu_custom_call" | custom-call | tf_op jit(solution)/shard_map/pallas_call | solution.py:357
  56.8 3.8 %collective-permute-start.1 = (bf16[2048,128]{1,0:T(8,128)(2,1)S(1)}, bf16[2048,128]{1,0:T(8,128)(2,1)}, u32[]{:S(2)}, u32[]{:S(2)}) collective-permute-start(bf16[2048,128]{1,0:T(8,128)(2,1)S(1)} %get-tuple-element.37), channel_id=1, source_target_pairs={{0,2},{2,4},{4,6},{6,8},{8,10},{10,12},{12,14},{1,3},{3,5},{5,7},{... | collective-permute-start | bytes 1572872 | tf_op jit(solution)/shard_map/ppermute | solution.py:247
  60.6 10.7 %collective-permute-done.1 = bf16[2048,128]{1,0:T(8,128)(2,1)} collective-permute-done((bf16[2048,128]{1,0:T(8,128)(2,1)S(1)}, bf16[2048,128]{1,0:T(8,128)(2,1)}, u32[]{:S(2)}, u32[]{:S(2)}) %collective-permute-start.1) | collective-permute-done | bytes 524320 | tf_op jit(solution)/shard_map/ppermute | solution.py:247
  71.3 5.3 %collective-permute-start.2 = (bf16[2048,128]{1,0:T(8,128)(2,1)}, bf16[2048,128]{1,0:T(8,128)(2,1)}, u32[]{:S(2)}, u32[]{:S(2)}) collective-permute-start(bf16[2048,128]{1,0:T(8,128)(2,1)} %collective-permute-done.1), channel_id=1, source_target_pairs={{0,2},{2,4},{4,6},{6,8},{8,10},{10,12},{12,14},{1,3},{3,5},{5,7},{... | collective-permute-start | bytes 1572872 | tf_op jit(solution)/shard_map/ppermute | solution.py:247
  77.2 24.0 %all-gather = f32[8,1,32]{2,1,0:T(1,128)S(1)} all-gather(f32[1,1,32]{2,1,0:T(1,128)S(1)} %slice_bitcast_fusion.2), channel_id=1, replica_groups=mesh['group'=2,'ctx'=8,'tp'=2] {'ctx'}, dimensions={0}, use_global_device_ids=true | all-gather | bytes 1152 | tf_op jit(solution)/shard_map/all_gather | solution.py:324
  101.9 2.3 add_convert_fusion.5
  107.4 3.7 %all-to-all-start.4 = ((bf16[128,2,2048]{2,0,1:T(8,128)(2,1)}), bf16[128,2,2048]{2,0,1:T(8,128)(2,1)S(1)}, u32[]{:S(2)}, u32[]{:S(2)}) async-start(bf16[128,2,2048]{2,0,1:T(8,128)(2,1)} %bitcast.173), calls=%async_computation.4 | async-start | bytes 2097152 | tf_op jit(solution)/shard_map/all_to_all | solution.py:281
  115.5 2.8 collective-permute-start.4
  120.6 8.3 %collective-permute-done.4 = bf16[2048,128]{1,0:T(8,128)(2,1)S(1)} collective-permute-done((bf16[2048,128]{1,0:T(8,128)(2,1)S(1)}, bf16[2048,128]{1,0:T(8,128)(2,1)S(1)}, u32[]{:S(2)}, u32[]{:S(2)}) %collective-permute-start.4) | collective-permute-done | bytes 524320 | tf_op jit(solution)/shard_map/ppermute | solution.py:247
  135.1 8.8 %shard_map.200 = (f32[256,2048]{1,0:T(8,128)S(1)}, f32[256,128]{1,0:T(8,128)S(1)}, f32[256,128]{1,0:T(8,128)S(1)}) custom-call(bf16[256,2048]{1,0:T(8,128)(2,1)S(1)} %copy-done.2, bf16[256,256]{1,0:T(8,128)(2,1)S(1)} %copy-done.18, bf16[256,256]{1,0:T(8,128)(2,1)S(1)} %copy-done.31, bf16[256,2048]{1,0:T(8,128)(2,1)S(1)} %bitcast.159, ...), custom_call_target="tpu_custom_call" | custom-call | tf_op jit(solution)/shard_map/pallas_call | solution.py:372
  148.6 2.5 psum.7
  159.4 29.0 %shard_map.201 = (bf16[256,2048]{1,0:T(8,128)(2,1)S(1)}, f32[256,2048]{1,0:T(8,128)S(1)}, f32[256,256]{1,0:T(8,128)S(1)}, f32[256,256]{1,0:T(8,128)S(1)}, bf16[2...) custom-call(bf16[256,2048]{1,0:T(8,128)(2,1)S(1)} %copy-done.3, ...), custom_call_target="tpu_custom_call" | custom-call | tf_op jit(solution)/shard_map/pallas_call | solution.py:392
  195.6 15.1 %collective-permute-done.5 = bf16[2048,128]{1,0:T(8,128)(2,1)} collective-permute-done((bf16[2048,128]{1,0:T(8,128)(2,1)S(1)}, bf16[2048,128]{1,0:T(8,128)(2,1)}, u32[]{:S(2)}, u32[]{:S(2)}) %collective-permute-start.5) | collective-permute-done | bytes 524320 | tf_op jit(solution)/shard_map/ppermute | solution.py:247
  212.1 22.3 %collective-permute-done.6 = bf16[2048,128]{1,0:T(8,128)(2,1)} collective-permute-done((bf16[2048,128]{1,0:T(8,128)(2,1)}, bf16[2048,128]{1,0:T(8,128)(2,1)}, u32[]{:S(2)}, u32[]{:S(2)}) %collective-permute-start.6) | collective-permute-done | bytes 524320 | tf_op jit(solution)/shard_map/ppermute | solution.py:247
  234.4 2.3 add_convert_fusion.2
  238.3 4.6 %all_to_all.184 = bf16[2,128,2048]{2,1,0:T(8,128)(2,1)S(1)} all-to-all(bf16[2,128,2048]{2,1,0:T(8,128)(2,1)S(1)} %bitcast.164), channel_id=1, replica_groups=mesh['group'=2,'ctx'=8,'tp'=2] {'tp'}, dimensions={0} | all-to-all | bytes 2097152 | tf_op jit(solution)/shard_map/all_to_all | solution.py:284
  245.6 7.2 %collective-permute-done.7 = bf16[2048,128]{1,0:T(8,128)(2,1)} collective-permute-done((bf16[2048,128]{1,0:T(8,128)(2,1)}, bf16[2048,128]{1,0:T(8,128)(2,1)}, u32[]{:S(2)}, u32[]{:S(2)}) %collective-permute-start.7) | collective-permute-done | bytes 524320 | tf_op jit(solution)/shard_map/ppermute | solution.py:247
  252.8 2.3 add_convert_fusion.1
  256.5 3.2 slice_bitcast_fusion
  259.7 2.9 copy.145
  266.0 15.4 %collective-permute-done.8 = bf16[2048,128]{1,0:T(8,128)(2,1)} collective-permute-done((bf16[2048,128]{1,0:T(8,128)(2,1)}, bf16[2048,128]{1,0:T(8,128)(2,1)}, u32[]{:S(2)}, u32[]{:S(2)}) %collective-permute-start.8) | collective-permute-done | bytes 524320 | tf_op jit(solution)/shard_map/ppermute | solution.py:247
  291.0 15.0 %shard_map.202 = (bf16[256,2048]{1,0:T(8,128)(2,1)S(1)}, bf16[256,256]{1,0:T(8,128)(2,1)S(1)}, bf16[256,256]{1,0:T(8,128)(2,1)S(1)}, f32[8,2048]{1,0:T(8,128)S(1...) custom-call(bf16[256,2048]{1,0:T(8,128)(2,1)S(1)} %copy-done.4, ...), custom_call_target="tpu_custom_call" | custom-call | tf_op jit(solution)/shard_map/pallas_call | solution.py:408
  311.8 2.3 copy.143
  316.7 3.7 %all_to_all.185 = bf16[2,128,32]{1,2,0:T(8,128)(2,1)S(1)} all-to-all(bf16[2,128,32]{1,2,0:T(8,128)(2,1)S(1)} %copy.149), channel_id=1, replica_groups=mesh['group'=2,'ctx'=8,'tp'=2] {'tp'}, dimensions={0} | all-to-all | bytes 32768 | tf_op jit(solution)/shard_map/all_to_all | solution.py:284
  320.8 4.7 %all_to_all.186 = bf16[2,128,2048]{2,1,0:T(8,128)(2,1)S(1)} all-to-all(bf16[2,128,2048]{2,1,0:T(8,128)(2,1)S(1)} %bitcast.163), channel_id=1, replica_groups=mesh['group'=2,'ctx'=8,'tp'=2] {'tp'}, dimensions={0} | all-to-all | bytes 2097152 | tf_op jit(solution)/shard_map/all_to_all | solution.py:284
  326.6 3.8 %all_to_all.187 = bf16[2,128,256]{2,1,0:T(8,128)(2,1)S(1)} all-to-all(bf16[2,128,256]{2,1,0:T(8,128)(2,1)S(1)} %bitcast.170), channel_id=1, replica_groups=mesh['group'=2,'ctx'=8,'tp'=2] {'tp'}, dimensions={0} | all-to-all | bytes 262144 | tf_op jit(solution)/shard_map/all_to_all | solution.py:284
  331.2 3.8 %all_to_all.188 = bf16[2,128,256]{2,1,0:T(8,128)(2,1)S(1)} all-to-all(bf16[2,128,256]{2,1,0:T(8,128)(2,1)S(1)} %bitcast.169), channel_id=1, replica_groups=mesh['group'=2,'ctx'=8,'tp'=2] {'tp'}, dimensions={0} | all-to-all | bytes 262144 | tf_op jit(solution)/shard_map/all_to_all | solution.py:284
  (272 shorter events, 94.1 us)
Async XLA Ops:
  0.6 36.7 %copy-start = (f32[4,4096]{1,0:T(4,128)S(1)}, f32[4,4096]{1,0:T(4,128)}, u32[]{:S(2)}) copy-start(f32[4,4096]{1,0:T(4,128)} %param.21) | copy-start | bytes 196612
  2.3 6.4 %all-to-all-start.2 = ((bf16[128,2,256]{2,0,1:T(8,128)(2,1)}), bf16[128,2,256]{2,0,1:T(8,128)(2,1)S(1)}, u32[]{:S(2)}, u32[]{:S(2)}) async-start(bf16[128,2,256]{2,0,1:T(8,128)(2,1)} %bitcast.155), calls=%async_computation.2 | async-start | bytes 262144 | tf_op jit(solution)/shard_map/all_to_all | solution.py:281
  5.7 13.6 %copy-start.64 = (s32[256]{0:T(256)S(1)}, s32[256]{0:T(256)}, u32[]{:S(2)}) copy-start(s32[256]{0:T(256)} %param.29) | copy-start | bytes 3076
  5.7 27.6 %copy-start.73 = (f32[64]{0:T(128)S(1)}, f32[64]{0:T(128)}, u32[]{:S(2)}) copy-start(f32[64]{0:T(128)} %param.25) | copy-start | bytes 772
  5.7 27.6 %copy-start.74 = (f32[64]{0:T(128)S(1)}, f32[64]{0:T(128)}, u32[]{:S(2)}) copy-start(f32[64]{0:T(128)} %param.24) | copy-start | bytes 772
  8.7 4.8 %all-to-all-start.1 = ((bf16[128,2,256]{2,0,1:T(8,128)(2,1)}), bf16[128,2,256]{2,0,1:T(8,128)(2,1)S(1)}, u32[]{:S(2)}, u32[]{:S(2)}) async-start(bf16[128,2,256]{2,0,1:T(8,128)(2,1)} %bitcast.156), calls=%async_computation.1 | async-start | bytes 262144 | tf_op jit(solution)/shard_map/all_to_all | solution.py:281
  13.5 21.6 %copy-start.27 = (bf16[128,2,256]{2,0,1:T(8,128)(2,1)}, bf16[128,2,256]{2,0,1:T(8,128)(2,1)S(1)}, u32[]{:S(2)}) copy-start(bf16[128,2,256]{2,0,1:T(8,128)(2,1)S(1)} %all-to-all-done.1) | copy-start | bytes 393220
  13.5 5.7 %all-to-all-start = ((bf16[128,2,2048]{2,0,1:T(8,128)(2,1)}), bf16[128,2,2048]{2,0,1:T(8,128)(2,1)S(1)}, u32[]{:S(2)}, u32[]{:S(2)}) async-start(bf16[128,2,2048]{2,0,1:T(8,128)(2,1)} %bitcast.154), calls=%async_computation | async-start | bytes 2097152 | tf_op jit(solution)/shard_map/all_to_all | solution.py:281
  17.1 21.0 %copy-start.69 = (f32[4,512]{1,0:T(4,128)S(1)}, f32[4,512]{1,0:T(4,128)}, u32[]{:S(2)}) copy-start(f32[4,512]{1,0:T(4,128)} %param.23) | copy-start | bytes 24580
  17.1 20.9 %copy-start.70 = (f32[4,512]{1,0:T(4,128)S(1)}, f32[4,512]{1,0:T(4,128)}, u32[]{:S(2)}) copy-start(f32[4,512]{1,0:T(4,128)} %param.22) | copy-start | bytes 24580
  23.1 16.6 %collective-permute-start = (bf16[3,2560]{1,0:T(4,128)(2,1)}, bf16[3,2560]{1,0:T(4,128)(2,1)}, u32[]{:S(2)}, u32[]{:S(2)}) collective-permute-start(bf16[3,2560]{1,0:T(4,128)(2,1)} %maximum_multiply_fusion), channel_id=1, source_target_pairs={{0,2},{2,4},{4,6},{6,8},{8,10},{10,12},{12,14},{1,3},{3,5},{5,7},{... | collective-permute-start | bytes 46088 | tf_op jit(solution)/shard_map/ppermute | solution.py:247
  28.5 4.6 %all-to-all-start.3 = ((bf16[128,2,32]{0,2,1:T(8,128)(2,1)}), bf16[128,2,32]{0,2,1:T(8,128)(2,1)S(1)}, u32[]{:S(2)}, u32[]{:S(2)}) async-start(bf16[128,2,32]{0,2,1:T(8,128)(2,1)} %bitcast.12), calls=%async_computation.3 | async-start | bytes 32768 | tf_op jit(solution)/shard_map/all_to_all | solution.py:281
  56.8 49.5 %copy-start.55 = (bf16[128,4096]{1,0:T(8,128)(2,1)S(1)}, bf16[128,4096]{1,0:T(8,128)(2,1)}, u32[]{:S(2)}) copy-start(bf16[128,4096]{1,0:T(8,128)(2,1)} %param.19) | copy-start | bytes 3145732
  56.8 14.5 %collective-permute-start.1 = (bf16[2048,128]{1,0:T(8,128)(2,1)S(1)}, bf16[2048,128]{1,0:T(8,128)(2,1)}, u32[]{:S(2)}, u32[]{:S(2)}) collective-permute-start(bf16[2048,128]{1,0:T(8,128)(2,1)S(1)} %get-tuple-element.37), channel_id=1, source_target_pairs={{0,2},{2,4},{4,6},{6,8},{8,10},{10,12},{12,14},{1,3},{3,5},{5,7},{... | collective-permute-start | bytes 1572872 | tf_op jit(solution)/shard_map/ppermute | solution.py:247
  71.3 30.6 %collective-permute-start.2 = (bf16[2048,128]{1,0:T(8,128)(2,1)}, bf16[2048,128]{1,0:T(8,128)(2,1)}, u32[]{:S(2)}, u32[]{:S(2)}) collective-permute-start(bf16[2048,128]{1,0:T(8,128)(2,1)} %collective-permute-done.1), channel_id=1, source_target_pairs={{0,2},{2,4},{4,6},{6,8},{8,10},{10,12},{12,14},{1,3},{3,5},{5,7},{... | collective-permute-start | bytes 1572872 | tf_op jit(solution)/shard_map/ppermute | solution.py:247
  104.2 9.7 %collective-permute-start.3 = (bf16[2048,128]{1,0:T(8,128)(2,1)}, bf16[2048,128]{1,0:T(8,128)(2,1)}, u32[]{:S(2)}, u32[]{:S(2)}) collective-permute-start(bf16[2048,128]{1,0:T(8,128)(2,1)} %add_convert_fusion.5), channel_id=1, source_target_pairs={{0,4},{2,6},{4,8},{6,10},{8,12},{10,14},{1,5},{3,7},{5,9},{7,11},{... | collective-permute-start | bytes 1572872 | tf_op jit(solution)/shard_map/ppermute | solution.py:247
  107.4 11.0 %copy-start.62 = (f32[4096]{0:T(1024)S(1)}, f32[4096]{0:T(1024)}, u32[]{:S(2)}) copy-start(f32[4096]{0:T(1024)} %param.28) | copy-start | bytes 49156
  107.4 22.7 %all-to-all-start.4 = ((bf16[128,2,2048]{2,0,1:T(8,128)(2,1)}), bf16[128,2,2048]{2,0,1:T(8,128)(2,1)S(1)}, u32[]{:S(2)}, u32[]{:S(2)}) async-start(bf16[128,2,2048]{2,0,1:T(8,128)(2,1)} %bitcast.173), calls=%async_computation.4 | async-start | bytes 2097152 | tf_op jit(solution)/shard_map/all_to_all | solution.py:281
  115.5 13.4 %collective-permute-start.4 = (bf16[2048,128]{1,0:T(8,128)(2,1)S(1)}, bf16[2048,128]{1,0:T(8,128)(2,1)S(1)}, u32[]{:S(2)}, u32[]{:S(2)}) collective-permute-start(bf16[2048,128]{1,0:T(8,128)(2,1)S(1)} %add_convert_fusion.4), channel_id=1, source_target_pairs={{0,8},{2,10},{4,12},{6,14},{1,9},{3,11},{5,13},{7,15},{16,24},{18,... | collective-permute-start | bytes 1572872 | tf_op jit(solution)/shard_map/ppermute | solution.py:247
  135.1 16.0 %copy-start.63 = (f32[256]{0:T(256)S(1)}, f32[256]{0:T(256)}, u32[]{:S(2)}) copy-start(f32[256]{0:T(256)} %select_reduce_fusion) | copy-start | bytes 3076
  159.4 52.6 %copy-start.68 = (f32[32]{0:T(128)S(1)}, f32[32]{0:T(128)}, u32[]{:S(2)}) copy-start(f32[32]{0:T(128)} %get-tuple-element.64) | copy-start | bytes 388
  159.4 78.6 %copy-start.67 = (f32[32]{0:T(128)S(1)}, f32[32]{0:T(128)}, u32[]{:S(2)}) copy-start(f32[32]{0:T(128)} %get-tuple-element.63) | copy-start | bytes 388
  159.4 78.8 %copy-start.66 = (f32[32]{0:T(128)S(1)}, f32[32]{0:T(128)}, u32[]{:S(2)}) copy-start(f32[32]{0:T(128)} %get-tuple-element.62) | copy-start | bytes 388
  194.1 44.2 %copy-start.26 = (bf16[256,2048]{1,0:T(8,128)(2,1)S(1)}, bf16[256,2048]{1,0:T(8,128)(2,1)}, u32[]{:S(2)}) copy-start(bf16[256,2048]{1,0:T(8,128)(2,1)} %copy-done.25) | copy-start | bytes 3145732
  194.1 16.5 %collective-permute-start.5 = (bf16[2048,128]{1,0:T(8,128)(2,1)S(1)}, bf16[2048,128]{1,0:T(8,128)(2,1)}, u32[]{:S(2)}, u32[]{:S(2)}) collective-permute-start(bf16[2048,128]{1,0:T(8,128)(2,1)S(1)} %get-tuple-element.41), channel_id=1, source_target_pairs={{2,0},{4,2},{6,4},{8,6},{10,8},{12,10},{14,12},{3,1},{5,3},{7,5},{... | collective-permute-start | bytes 1572872 | tf_op jit(solution)/shard_map/ppermute | solution.py:247
  210.6 23.7 %collective-permute-start.6 = (bf16[2048,128]{1,0:T(8,128)(2,1)}, bf16[2048,128]{1,0:T(8,128)(2,1)}, u32[]{:S(2)}, u32[]{:S(2)}) collective-permute-start(bf16[2048,128]{1,0:T(8,128)(2,1)} %collective-permute-done.5), channel_id=1, source_target_pairs={{2,0},{4,2},{6,4},{8,6},{10,8},{12,10},{14,12},{3,1},{5,3},{7,5},{... | collective-permute-start | bytes 1572872 | tf_op jit(solution)/shard_map/ppermute | solution.py:247
  236.7 16.1 %collective-permute-start.7 = (bf16[2048,128]{1,0:T(8,128)(2,1)}, bf16[2048,128]{1,0:T(8,128)(2,1)}, u32[]{:S(2)}, u32[]{:S(2)}) collective-permute-start(bf16[2048,128]{1,0:T(8,128)(2,1)} %add_convert_fusion.2), channel_id=1, source_target_pairs={{4,0},{6,2},{8,4},{10,6},{12,8},{14,10},{5,1},{7,3},{9,5},{11,7},{... | collective-permute-start | bytes 1572872 | tf_op jit(solution)/shard_map/ppermute | solution.py:247
  255.2 26.2 %collective-permute-start.8 = (bf16[2048,128]{1,0:T(8,128)(2,1)}, bf16[2048,128]{1,0:T(8,128)(2,1)}, u32[]{:S(2)}, u32[]{:S(2)}) collective-permute-start(bf16[2048,128]{1,0:T(8,128)(2,1)} %add_convert_fusion.1), channel_id=1, source_target_pairs={{8,0},{10,2},{12,4},{14,6},{9,1},{11,3},{13,5},{15,7},{24,16},{26,... | collective-permute-start | bytes 1572872 | tf_op jit(solution)/shard_map/ppermute | solution.py:247
  259.7 23.3 %copy-start.4 = (bf16[256,2048]{1,0:T(8,128)(2,1)S(1)}, bf16[256,2048]{1,0:T(8,128)(2,1)}, u32[]{:S(2)}) copy-start(bf16[256,2048]{1,0:T(8,128)(2,1)} %copy-done.1) | copy-start | bytes 3145732
  259.7 23.3 %copy-start.16 = (f32[256,8]{1,0:T(8,128)S(1)}, f32[256,8]{1,0:T(8,128)}, u32[]{:S(2)}) copy-start(f32[256,8]{1,0:T(8,128)} %copy-done.15) | copy-start | bytes 24580
  259.7 23.3 %copy-start.20 = (bf16[256,256]{1,0:T(8,128)(2,1)S(1)}, bf16[256,256]{1,0:T(8,128)(2,1)}, u32[]{:S(2)}) copy-start(bf16[256,256]{1,0:T(8,128)(2,1)} %copy-done.17) | copy-start | bytes 393220
  308.9 11.5 %collective-permute-start.9 = (f32[3,2560]{1,0:T(4,128)S(1)}, f32[3,2560]{1,0:T(4,128)S(1)}, u32[]{:S(2)}, u32[]{:S(2)}) collective-permute-start(f32[3,2560]{1,0:T(4,128)S(1)} %pad_maximum_fusion.1), channel_id=1, source_target_pairs={{2,0},{4,2},{6,4},{8,6},{10,8},{12,10},{14,12},{3,1},{5,3},{7,5},{... | collective-permute-start | bytes 92168 | tf_op jit(solution)/shard_map/ppermute | solution.py:247
  (58 other events, 126.2 us)

commit v2 on v1

--- a/solution.py
+++ b/solution.py
@@ -1,3 +1,5 @@
+from functools import partial
+
 import jax
 import jax.numpy as jnp
 from jax import lax
@@ -247,26 +249,167 @@
     return lax.ppermute(value, "ctx", [(i, i + steps) for i in range(initial, last)])
 
 
-def carry(states, decays, sign):
+MESH = pl.DeviceIdType.MESH
+CHUNKS = 4
+
+
+def carry_kernel(sign, count, s_ref, mine_ref, peer_ref, out, other, came, going, sems):
+    me = lax.axis_index("ctx")
+    half = lax.rem(me, 2)
+    pair = lax.div(me, 2)
+    pairs = count // 2
+    peer = me + 1 - 2 * half
+    is_first = half == (0 if sign > 0 else 1)
+    has_prev = (pair > 0) if sign > 0 else (pair < pairs - 1)
+    has_next = (pair < pairs - 1) if sign > 0 else (pair > 0)
+    heads = s_ref.shape[0]
+    step = heads // CHUNKS
+
+    barrier = pltpu.get_barrier_semaphore()
+    pl.semaphore_signal(barrier, inc=1, device_id={"ctx": peer}, device_id_type=MESH)
+
+    @pl.when(has_prev)
+    def _():
+        pl.semaphore_signal(barrier, inc=1, device_id={"ctx": me - 2 * sign}, device_id_type=MESH)
+
+    @pl.when(has_next)
+    def _():
+        pl.semaphore_signal(barrier, inc=1, device_id={"ctx": me + 2 * sign}, device_id_type=MESH)
+
+    pl.semaphore_wait(barrier, 1 + jnp.where(has_prev, 1, 0) + jnp.where(has_next, 1, 0))
+
+    def swap(i):
+        part = pl.ds(i * step, step)
+        return pltpu.make_async_remote_copy(
+            src_ref=s_ref.at[part], dst_ref=other.at[part], send_sem=sems.at[0, i],
+            recv_sem=sems.at[1, i], device_id={"ctx": peer}, device_id_type=MESH,
+        )
+
+    def chain(i):
+        part = pl.ds(i * step, step)
+        return pltpu.make_async_remote_copy(
+            src_ref=going.at[part], dst_ref=came.at[part], send_sem=sems.at[2, i],
+            recv_sem=sems.at[3, i], device_id={"ctx": me + 2 * sign}, device_id_type=MESH,
+        )
+
+    for i in range(CHUNKS):
+        swap(i).start()
+
+    @pl.when(jnp.logical_not(has_prev))
+    def _():
+        came[...] = jnp.zeros(came.shape, bf16)
+
+    for i in range(CHUNKS):
+        part = slice(i * step, (i + 1) * step)
+        swap(i).wait_recv()
+
+        @pl.when(has_prev)
+        def _():
+            chain(i).wait_recv()
+
+        base = came[part].astype(f32)
+        own, got = s_ref[part].astype(f32), other[part].astype(f32)
+        d_own, d_got = mine_ref[part], peer_ref[part]
+
+        @pl.when(is_first)
+        def _():
+            out[part] = came[part]
+            going[part] = (d_got * (d_own * base + own) + got).astype(bf16)
+
+        @pl.when(jnp.logical_not(is_first))
+        def _():
+            mid = d_got * base + got
+            out[part] = mid.astype(bf16)
+            going[part] = (d_own * mid + own).astype(bf16)
+
+        @pl.when(has_next)
+        def _():
+            chain(i).start()
+
+    for i in range(CHUNKS):
+        swap(i).wait_send()
+
+        @pl.when(has_next)
+        def _():
+            chain(i).wait_send()
+
+
+def carry(states, mine_decay, peer_decay, sign):
     count = lax.axis_size("ctx")
-    me = lax.axis_index("ctx")
-    heads = decays.shape[1]
-    shape3 = (heads, HEAD_DIM, STATE)
-    held = hop(states, sign)
-    span = 1
-    while span < count - 1:
-        prod = jnp.ones((heads,), f32)
-        for i in range(1, span + 1):
-            prod = prod * lax.dynamic_index_in_dim(
-                decays, jnp.clip(me - sign * i, 0, count - 1), 0, False
-            )
-        got = hop(held, sign * span)
-        total = prod[:, None, None] * got.astype(f32).reshape(shape3) + held.astype(f32).reshape(
-            shape3
+    heads = states.shape[0] // HEAD_DIM
+    shape = (heads, HEAD_DIM, STATE)
+    vmem = pl.BlockSpec(memory_space=pltpu.VMEM)
+    out = pl.pallas_call(
+        partial(carry_kernel, sign, count),
+        out_shape=jax.ShapeDtypeStruct(shape, bf16),
+        in_specs=[vmem] * 3,
+        out_specs=vmem,
+        scratch_shapes=[
+            pltpu.VMEM(shape, bf16), pltpu.VMEM(shape, bf16), pltpu.VMEM(shape, bf16),
+            pltpu.SemaphoreType.DMA((4, CHUNKS)),
+        ],
+        compiler_params=pltpu.CompilerParams(
+            collective_id=0 if sign > 0 else 1, has_side_effects=True,
+            vmem_limit_bytes=32 * 1024 * 1024,
+        ),
+    )(states.reshape(shape), mine_decay, peer_decay)
+    return out.reshape(states.shape)
+
+
+def swap_barrier(peer):
+    barrier = pltpu.get_barrier_semaphore()
+    pl.semaphore_signal(barrier, inc=1, device_id={"tp": peer}, device_id_type=MESH)
+    pl.semaphore_wait(barrier, 1)
+
+
+def move_kernel(to_heads, count, *refs):
+    ins, outs, sems = refs[:count], refs[count : 2 * count], refs[2 * count]
+    me = lax.axis_index("tp")
+    peer = 1 - me
+    swap_barrier(peer)
+    copies = []
+    for i in range(count):
+        a, o = ins[i], outs[i]
+        if to_heads:
+            rows, width = a.shape[0], o.shape[1]
+            there = pl.ds(pl.multiple_of(peer * width, 128), width)
+            here = pl.ds(pl.multiple_of(me * width, 128), width)
+            place = pl.ds(pl.multiple_of(me * rows, 8), rows)
+            send, keep, dst = a.at[:, there], a.at[:, here], o.at[place, :]
+        else:
+            rows, width = o.shape[0], a.shape[1]
+            there = pl.ds(pl.multiple_of(peer * rows, 8), rows)
+            here = pl.ds(pl.multiple_of(me * rows, 8), rows)
+            place = pl.ds(pl.multiple_of(me * width, 128), width)
+            send, keep, dst = a.at[there, :], a.at[here, :], o.at[:, place]
+        away = pltpu.make_async_remote_copy(
+            src_ref=send, dst_ref=dst, send_sem=sems.at[0, i], recv_sem=sems.at[1, i],
+            device_id={"tp": peer}, device_id_type=MESH,
         )
-        held = total.reshape(states.shape).astype(bf16)
-        span *= 2
-    return held
+        away.start()
+        local = pltpu.make_async_copy(keep, dst, sems.at[2, i])
+        local.start()
+        copies.append((away, local))
+    for away, local in copies:
+        away.wait()
+        local.wait()
+
+
+def move(arrays, to_heads, collective):
+    count = len(arrays)
+    anywhere = pl.BlockSpec(memory_space=pl.ANY)
+    shapes = []
+    for a in arrays:
+        r, w = a.shape
+        shapes.append(jax.ShapeDtypeStruct((2 * r, w // 2) if to_heads else (r // 2, 2 * w), a.dtype))
+    return pl.pallas_call(
+        partial(move_kernel, to_heads, count),
+        out_shape=shapes,
+        in_specs=[anywhere] * count,
+        out_specs=[anywhere] * count,
+        scratch_shapes=[pltpu.SemaphoreType.DMA((3, count))],
+        compiler_params=pltpu.CompilerParams(collective_id=collective, has_side_effects=True),
+    )(*arrays)
 
 
 def shards(
@@ -277,14 +420,13 @@
     tp = lax.axis_index("tp")
     tpn = lax.axis_size("tp")
 
-    def fwd(a):
-        return lax.all_to_all(a, "tp", split_axis=1, concat_axis=0, tiled=True)
-
-    def rev(a):
-        return lax.all_to_all(a, "tp", split_axis=0, concat_axis=1, tiled=True)
-
-    dt_in = fwd(dt_raw).astype(f32)
-    x, b, c, z = fwd(x_in), fwd(b_in), fwd(c_in), fwd(z_in)
+    part_heads = dt_raw.shape[1] // tpn
+    lanes = ((0, 0), (0, 128 - part_heads))
+    dt_wide = jnp.concatenate(
+        [jnp.pad(dt_raw[:, :part_heads], lanes), jnp.pad(dt_raw[:, part_heads:], lanes)], axis=1
+    )
+    x, b, c, z, dt_got = move([x_in, b_in, c_in, z_in, dt_wide], True, 2)
+    dt_in = dt_got[:, :part_heads].astype(f32)
     T = x.shape[0]
     W, N, H = x.shape[1], b.shape[1], dt_in.shape[1]
     pairs = H // 2
@@ -321,7 +463,10 @@
     tail_decay = jnp.exp(cum[-1][None, :] - cum) * jnp.where(counts == counts[-1], 1.0, 0.0)[:, None]
     we = tail_decay * dt
     decay = reach[-1]
-    decays = lax.all_gather(decay, "ctx")
+    count = lax.axis_size("ctx")
+    peer = lax.ppermute(decay, "ctx", [(i, i ^ 1) for i in range(count)])
+    mine_decay = jnp.broadcast_to(decay[:, None, None], (H, 1, STATE))
+    peer_decay = jnp.broadcast_to(peer[:, None, None], (H, 1, STATE))
 
     def to_pairs(a):
         return a.reshape(T, pairs, 2).transpose(1, 0, 2)
@@ -367,7 +512,7 @@
         compiler_params=params,
     )(x, b, c, tx, tb, tc, wx, wb, wc, valid, cols)
 
-    state = carry(add, decays, 1)
+    state = carry(add, mine_decay, peer_decay, 1)
 
     mixed, squares, numer = pl.pallas_call(
         mix_kernel,
@@ -402,8 +547,7 @@
         compiler_params=params,
     )(xc, bc, cc, z, state, cols, rowvals, seg, gw, skip_row, mixed, vcols)
 
-    grad_z = rev(dz)
-    gstate = carry(ds, decays, -1)
+    gstate = carry(ds, mine_decay, peer_decay, -1)
 
     gx, gb, gc, hx, hb, hc, lx, lb, lc, stats, inner = pl.pallas_call(
         last_kernel,
@@ -431,7 +575,7 @@
     at_end = jnp.sum(tail_part, axis=0) + decay * ginner
     rev_sum = jnp.dot(lower.T, dcum, precision=highest) + at_end[None, :]
     ddt = col_sum + tail_decay * xg - rate[None, :] * rev_sum
-    grad_dt = rev((ddt * jax.nn.sigmoid(dt_pre)).astype(bf16))
+    ddt_wide = jnp.pad((ddt * jax.nn.sigmoid(dt_pre)).astype(bf16), lanes)
 
     heads3 = jnp.concatenate([hx, hb, hc], axis=1)[5:8]
     last3 = jnp.concatenate([lx, lb, lc], axis=1)[5:8]
@@ -440,7 +584,9 @@
     gb = lax.dynamic_update_slice(gb, fixed[:, W : W + N], (T - 3, 0))
     gc = lax.dynamic_update_slice(gc, fixed[:, W + N :], (T - 3, 0))
     out_values = lax.dynamic_slice_in_dim(values, tp * tok, tok, 0)
-    return (out_values, rev(gx), rev(gb), rev(gc), grad_z, grad_dt)
+    grad_x, grad_b, grad_c, grad_z, dt_out = move([gx, gb, gc, dz, ddt_wide], False, 3)
+    grad_dt = jnp.concatenate([dt_out[:, :part_heads], dt_out[:, 128 : 128 + part_heads]], axis=1)
+    return (out_values, grad_x, grad_b, grad_c, grad_z, grad_dt)
 
 
 def r8s(width):

time: 340 us -> 281 us (0.83)
  Pallas kernels: 62.6 us -> 197 us
  waiting for transfers between devices: 83.9 us -> 0.01 us
  blocking collectives: 47.2 us -> 3.15 us
  starting transfers between devices: 43.3 us -> 7.29 us
  local copies, waits for them, and re-layouts: 70.1 us -> 51.5 us
  other arithmetic: 25.1 us -> 15.8 us
    pallas_call x0 -> x4, Pallas kernels: none -> 134 us  [the longest x2 76.4 us: move(): pl.pallas_call(partial(move_kernel, to_heads, count), out_shape=shapes, i...]
    ppermute x10 -> x2, waiting for transfers between devices: 79 us -> 0.01 us  [hop(): lax.ppermute(value, 'ctx', [(i, i + steps) for i in range(initial, last)])]
    all_gather x1 -> x0, blocking collectives: 24 us -> none  [shards(): decays = lax.all_gather(decay, 'ctx')]
    all_to_all x5 -> x0, blocking collectives: 20.7 us -> none  [rev(): return lax.all_to_all(a, 'tp', split_axis=0, concat_axis=1, tiled=True)]
    ppermute x10 -> x2, starting transfers between devices: 26 us -> 5.7 us  [hop(): lax.ppermute(value, 'ctx', [(i, i + steps) for i in range(initial, last)])]
    all_to_all x5 -> x0, starting transfers between devices: 17.3 us -> none  [fwd(): return lax.all_to_all(a, 'tp', split_axis=1, concat_axis=0, tiled=True)]
    unnamed x153 -> x148, local copies, waits for them, and re-layouts: 39.5 us -> 26.2 us
    convert_element_type x7 -> x0, other arithmetic: 11.3 us -> none  [the longest x6 11.2 us: carry(): held = total.reshape(states.shape).astype(bf16)]
  transfers between devices with their start and end apart: 15 -> 3, of which waited for: 9 -> 0; matrix products, arithmetic and copies ran while one was open for 11% -> 7% of each run, Pallas kernels for 0% -> 4%
where the time goes in v2:
time: 281 us; the launch traced here: 279 us
  Pallas kernels  197 us (70%)
  local copies, waits for them, and re-layouts  51.5 us (18%)
  other arithmetic  15.8 us (6%)
  starting transfers between devices  7.29 us (3%)
  between operations  3.49 us (1%)
  blocking collectives  3.15 us (1%)
    pallas_call x2, Pallas kernels, move(): pl.pallas_call(partial(move_kernel, to_heads, count), out_shape=shapes, i...  76.4 us
    pallas_call x2, Pallas kernels, carry(): pl.pallas_call(partial(carry_kernel, sign, count), out_shape=jax.ShapeDty...  57.7 us
    pallas_call x1, Pallas kernels, shards(): pl.pallas_call(back_kernel, grid=(pairs,), in_specs=[px, pg, pg, px, st,...  29.1 us
    unnamed x148, local copies, waits for them, and re-layouts  26.2 us
    pallas_call x1, Pallas kernels, shards(): pl.pallas_call(last_kernel, grid=(pairs,), in_specs=[px, pg, st, st, c8,...  15 us
    pallas_call x1, Pallas kernels, shards(): pl.pallas_call(conv_kernel, grid=(pairs,), in_specs=[px, pg, pg, t8x, t8g...  9.82 us
    transpose x4, local copies, waits for them, and re-layouts, from_cols(): return a[:, :, :2].transpose(1, 0, 2).reshape(T, H)  9.29 us
    pallas_call x1, Pallas kernels, shards(): pl.pallas_call(mix_kernel, grid=(pairs,), in_specs=[px, pg, pg, px, st, c...  8.76 us
  transfers between devices with their start and end apart: 3, of which 0 were waited for; matrix products, arithmetic and copies ran while one was open for 7% of the time, Pallas kernels for 4%

profile of v2, /device:TPU:0, one launch (start us, length us, event | category | flops | bytes accessed | tf_op | source)
XLA Modules:
  0.0 278.8 jit_solution(11852687309147179950)
XLA Ops:
  5.5 38.4 %shard_map.199 = (bf16[256,2048]{1,0:T(8,128)(2,1)}, bf16[256,256]{1,0:T(8,128)(2,1)}, bf16[256,256]{1,0:T(8,128)(2,1)}, bf16[256,2048]{1,0:T(8,128)(2,1)}, bf16[256,128]{1,0:T(8,128)(2,1)}) custom-call(bf16[128,4096]{1,0:T(8,128)(2,1)} %refs_0_.1, bf16[128,512]{1,0:T(8,128)(2,1)} %refs_1_.1, bf16[128,512]{1,0:T(8,128)(2,1)} %refs_2_.1, ...), custom_call_target="tpu_custom_call" | custom-call | tf_op jit(solution)/shard_map/pallas_call | solution.py:405
  46.9 4.4 %collective-permute-start = (bf16[3,2560]{1,0:T(4,128)(2,1)S(1)}, bf16[3,2560]{1,0:T(4,128)(2,1)S(1)}, u32[]{:S(2)}, u32[]{:S(2)}) collective-permute-start(bf16[3,2560]{1,0:T(4,128)(2,1)S(1)} %maximum_multiply_fusion), channel_id=1, source_target_pairs={{0,2},{2,4},{4,6},{6,8},{8,10},{10,12},{12,14},{1,3},{3,5},{5,7},{... | collective-permute-start | bytes 46088 | tf_op jit(solution)/shard_map/ppermute | solution.py:249
  55.5 1.6 collective-permute-start.1
  65.2 9.8 %shard_map.200 = (bf16[256,2048]{1,0:T(8,128)(2,1)S(1)}, bf16[256,256]{1,0:T(8,128)(2,1)S(1)}, bf16[256,256]{1,0:T(8,128)(2,1)S(1)}, f32[256,2048]{1,0:T(8,128)S...) custom-call(bf16[256,2048]{1,0:T(8,128)(2,1)S(1)} %copy-done.19, ...), custom_call_target="tpu_custom_call" | custom-call | tf_op jit(solution)/shard_map/pallas_call | solution.py:502
  75.0 1.3 copy-done.9
  77.3 17.6 %shard_map.201 = bf16[32,64,128]{2,1,0:T(8,128)(2,1)S(1)} custom-call(bf16[32,64,128]{2,1,0:T(8,128)(2,1)S(1)} %bitcast.77, f32[32,1,128]{2,1,0:T(1,128)S(1)} %broadcast_in_dim.69.mine_ref, f32[32,1,128]{2,1,0:T(1,128)S(1)} %broadcast_in_dim.70.peer_ref), custom_call_target="tpu_custom_call" | custom-call | tf_op jit(solution)/shard_map/pallas_call | solution.py:342
  95.0 8.8 %shard_map.202 = (f32[256,2048]{1,0:T(8,128)S(1)}, f32[256,128]{1,0:T(8,128)S(1)}, f32[256,128]{1,0:T(8,128)S(1)}) custom-call(bf16[256,2048]{1,0:T(8,128)(2,1)S(1)} %get-tuple-element.48.xc, bf16[256,256]{1,0:T(8,128)(2,1)S(1)} %get-tuple-element.49.bc, bf16[256,256]{1,0:T(8,128)(2,1)S(1)} %get-tuple-element.50.cc, bf16[256,2048]{1,0:T(8,128)(2,1)S(1)} %copy-done.4, ...), custom_call_target="tpu_custom_call" | custom-call | tf_op jit(solution)/shard_map/pallas_call | solution.py:517
  103.8 1.3 copy-done.11
  106.4 1.6 reduce_sum.49
  108.0 1.6 reduce_sum.50
  109.6 1.3 pad_maximum_fusion.6
  110.8 3.1 %psum.7 = f32[2,256]{1,0:T(2,128)} all-reduce(f32[2,256]{1,0:T(2,128)} %pad_maximum_fusion.6), channel_id=1, replica_groups=mesh['group'=2,'ctx'=8,'tp'=2] {'tp'}, use_global_device_ids=true, to_apply=%region_2.3 | all-reduce | flops 512 | bytes 4096 | tf_op jit(solution)/shard_map/psum | solution.py:527
  114.0 1.4 fusion.26
  115.3 1.3 fusion.25
  116.7 1.5 stack.50
  118.2 1.5 copy.111.vcols
  121.9 1.6 copy-done.12
  127.2 29.1 %shard_map.203 = (bf16[256,2048]{1,0:T(8,128)(2,1)S(1)}, f32[256,2048]{1,0:T(8,128)S(1)}, f32[256,256]{1,0:T(8,128)S(1)}, f32[256,256]{1,0:T(8,128)S(1)}, bf16[2...) custom-call(bf16[256,2048]{1,0:T(8,128)(2,1)S(1)} %get-tuple-element.48.xc, ...), custom_call_target="tpu_custom_call" | custom-call | tf_op jit(solution)/shard_map/pallas_call | solution.py:537
  156.2 1.3 copy-done.6
  157.6 40.1 %shard_map.204 = bf16[32,64,128]{2,1,0:T(8,128)(2,1)S(1)} custom-call(bf16[32,64,128]{2,1,0:T(8,128)(2,1)S(1)} %bitcast.78, f32[32,1,128]{2,1,0:T(1,128)S(1)} %broadcast_in_dim.69.mine_ref, f32[32,1,128]{2,1,0:T(1,128)S(1)} %broadcast_in_dim.70.peer_ref), custom_call_target="tpu_custom_call" | custom-call | tf_op jit(solution)/shard_map/pallas_call | solution.py:342
  197.8 15.0 %shard_map.205 = (bf16[256,2048]{1,0:T(8,128)(2,1)S(1)}, bf16[256,256]{1,0:T(8,128)(2,1)S(1)}, bf16[256,256]{1,0:T(8,128)(2,1)S(1)}, f32[8,2048]{1,0:T(8,128)S(1...) custom-call(bf16[256,2048]{1,0:T(8,128)(2,1)S(1)} %get-tuple-element, ...), custom_call_target="tpu_custom_call" | custom-call | tf_op jit(solution)/shard_map/pallas_call | solution.py:552
  212.8 1.3 copy-done.8
  217.0 1.3 collective-permute-start.2
  218.4 3.2 %slice_bitcast_fusion.1 = f32[256,16,2]{2,0,1:T(8,128)} fusion(f32[16,256,8]{2,1,0:T(8,128)} %copy-done.8), kind=kLoop, calls=%fused_computation.1 | loop fusion | bytes 65536 | tf_op jit(solution)/shard_map/transpose | solution.py:567
  221.5 2.4 copy.114
  224.1 1.5 slice_bitcast_fusion
  225.6 2.3 copy.116
  230.6 1.4 dynamic_update_slice.9.refs_0_
  232.0 1.3 dynamic_update_slice.11.refs_2_
  233.3 1.3 dynamic_update_slice.10.refs_1_
  234.6 38.0 %shard_map.206 = (bf16[128,4096]{1,0:T(8,128)(2,1)}, bf16[128,512]{1,0:T(8,128)(2,1)}, bf16[128,512]{1,0:T(8,128)(2,1)}, bf16[128,4096]{1,0:T(8,128)(2,1)}, bf16[128,256]{1,0:T(8,128)(2,1)}) custom-call(bf16[256,2048]{1,0:T(8,128)(2,1)} %dynamic_update_slice.9.refs_0_, bf16[256,256]{1,0:T(8,128)(2,1)} %dynamic_update_slice.10.refs_1_, ...), custom_call_target="tpu_custom_call" | custom-call | tf_op jit(solution)/shard_map/pallas_call | solution.py:405
  274.3 2.3 copy.133
  (218 shorter events, 35.5 us)
Async XLA Ops:
  0.6 58.8 %copy-start = (f32[4,4096]{1,0:T(4,128)S(1)}, f32[4,4096]{1,0:T(4,128)}, u32[]{:S(2)}) copy-start(f32[4,4096]{1,0:T(4,128)} %param.21) | copy-start | bytes 196612
  0.6 50.7 %copy-start.67 = (f32[64]{0:T(128)S(1)}, f32[64]{0:T(128)}, u32[]{:S(2)}) copy-start(f32[64]{0:T(128)} %param.25) | copy-start | bytes 772
  0.7 50.8 %copy-start.68 = (f32[64]{0:T(128)S(1)}, f32[64]{0:T(128)}, u32[]{:S(2)}) copy-start(f32[64]{0:T(128)} %param.24) | copy-start | bytes 772
  5.5 51.6 %copy-start.53 = (s32[256]{0:T(256)S(1)}, s32[256]{0:T(256)}, u32[]{:S(2)}) copy-start(s32[256]{0:T(256)} %param.29) | copy-start | bytes 3076
  44.0 14.7 %copy-start.61 = (f32[256]{0:T(256)S(1)}, f32[256]{0:T(256)}, u32[]{:S(2)}) copy-start(f32[256]{0:T(256)} %param.31) | copy-start | bytes 3076
  44.0 14.7 %copy-start.62 = (s32[256]{0:T(256)S(1)}, s32[256]{0:T(256)}, u32[]{:S(2)}) copy-start(s32[256]{0:T(256)} %param.30) | copy-start | bytes 3076
  44.0 15.4 %copy-start.51 = (f32[4096]{0:T(1024)S(1)}, f32[4096]{0:T(1024)}, u32[]{:S(2)}) copy-start(f32[4096]{0:T(1024)} %param.28) | copy-start | bytes 49156
  44.0 15.4 %copy-start.52 = (f32[4096]{0:T(1024)S(1)}, f32[4096]{0:T(1024)}, u32[]{:S(2)}) copy-start(f32[4096]{0:T(1024)} %param.27) | copy-start | bytes 49156
  44.0 16.2 %copy-start.57 = (f32[4,512]{1,0:T(4,128)S(1)}, f32[4,512]{1,0:T(4,128)}, u32[]{:S(2)}) copy-start(f32[4,512]{1,0:T(4,128)} %param.23) | copy-start | bytes 24580
  44.0 16.2 %copy-start.58 = (f32[4,512]{1,0:T(4,128)S(1)}, f32[4,512]{1,0:T(4,128)}, u32[]{:S(2)}) copy-start(f32[4,512]{1,0:T(4,128)} %param.22) | copy-start | bytes 24580
  44.0 16.3 %copy-start.69 = (f32[64]{0:T(128)S(1)}, f32[64]{0:T(128)}, u32[]{:S(2)}) copy-start(f32[64]{0:T(128)} %param.26) | copy-start | bytes 772
  46.9 14.3 %collective-permute-start = (bf16[3,2560]{1,0:T(4,128)(2,1)S(1)}, bf16[3,2560]{1,0:T(4,128)(2,1)S(1)}, u32[]{:S(2)}, u32[]{:S(2)}) collective-permute-start(bf16[3,2560]{1,0:T(4,128)(2,1)S(1)} %maximum_multiply_fusion), channel_id=1, source_target_pairs={{0,2},{2,4},{4,6},{6,8},{8,10},{10,12},{12,14},{1,3},{3,5},{5,7},{... | collective-permute-start | bytes 46088 | tf_op jit(solution)/shard_map/ppermute | solution.py:249
  55.5 21.6 %collective-permute-start.1 = (f32[32]{0:T(128)S(1)}, f32[32]{0:T(128)S(1)}, u32[]{:S(2)}, u32[]{:S(2)}) collective-permute-start(f32[32]{0:T(128)S(1)} %slice_bitcast_fusion.2), channel_id=1, source_target_pairs={{0,2},{2,0},{4,6},{6,4},{8,10},{10,8},{12,14},{14,12},{1,3},{3,1},... | collective-permute-start | bytes 392 | tf_op jit(solution)/shard_map/ppermute | solution.py:467
  60.3 14.7 %copy-start.37 = (f32[4,256]{1,0:T(4,128)}, f32[4,256]{1,0:T(4,128)S(1)}, u32[]{:S(2)}) copy-start(f32[4,256]{1,0:T(4,128)S(1)} %get-tuple-element.132.wc) | copy-start | bytes 12292
  60.3 14.7 %copy-start.39 = (f32[4,256]{1,0:T(4,128)}, f32[4,256]{1,0:T(4,128)S(1)}, u32[]{:S(2)}) copy-start(f32[4,256]{1,0:T(4,128)S(1)} %get-tuple-element.133.wb) | copy-start | bytes 12292
  61.2 16.0 %copy-start.66 = (f32[32]{0:T(128)S(1)}, f32[32]{0:T(128)}, u32[]{:S(2)}) copy-start(f32[32]{0:T(128)} %copy-done.65) | copy-start | bytes 388
  65.2 29.8 %copy-start.4 = (bf16[256,2048]{1,0:T(8,128)(2,1)S(1)}, bf16[256,2048]{1,0:T(8,128)(2,1)}, u32[]{:S(2)}) copy-start(bf16[256,2048]{1,0:T(8,128)(2,1)} %get-tuple-element.51.z) | copy-start | bytes 3145732
  65.2 29.8 %copy-start.17 = (f32[16,8,256]{2,1,0:T(8,128)S(1)}, f32[16,8,256]{2,1,0:T(8,128)}, u32[]{:S(2)}) copy-start(f32[16,8,256]{2,1,0:T(8,128)} %maximum_maximum_fusion.rows_ref) | copy-start | bytes 393220
  77.1 17.9 %copy-start.27 = (f32[256,256]{1,0:T(8,128)}, f32[256,256]{1,0:T(8,128)S(1)}, u32[]{:S(2)}) copy-start(f32[256,256]{1,0:T(8,128)S(1)} %get-tuple-element.62.uc) | copy-start | bytes 786436
  77.1 26.7 %copy-start.15 = (bf16[256,256]{1,0:T(8,128)(2,1)}, bf16[256,256]{1,0:T(8,128)(2,1)S(1)}, u32[]{:S(2)}) copy-start(bf16[256,256]{1,0:T(8,128)(2,1)S(1)} %get-tuple-element.49.bc) | copy-start | bytes 393220
  77.1 26.7 %copy-start.23 = (bf16[256,256]{1,0:T(8,128)(2,1)}, bf16[256,256]{1,0:T(8,128)(2,1)S(1)}, u32[]{:S(2)}) copy-start(bf16[256,256]{1,0:T(8,128)(2,1)S(1)} %get-tuple-element.50.cc) | copy-start | bytes 393220
  94.9 8.8 %copy-start.1 = (bf16[32,64,128]{2,1,0:T(8,128)(2,1)}, bf16[32,64,128]{2,1,0:T(8,128)(2,1)S(1)}, u32[]{:S(2)}) copy-start(bf16[32,64,128]{2,1,0:T(8,128)(2,1)S(1)} %shard_map.201) | copy-start | bytes 1572868
  127.1 70.6 %copy-start.3 = (bf16[32,64,128]{2,1,0:T(8,128)(2,1)S(1)}, bf16[32,64,128]{2,1,0:T(8,128)(2,1)}, u32[]{:S(2)}) copy-start(bf16[32,64,128]{2,1,0:T(8,128)(2,1)} %copy-done.1) | copy-start | bytes 1572868
  127.1 70.6 %copy-start.10 = (f32[256,2048]{1,0:T(8,128)S(1)}, f32[256,2048]{1,0:T(8,128)}, u32[]{:S(2)}) copy-start(f32[256,2048]{1,0:T(8,128)} %copy-done.9) | copy-start | bytes 6291460
  127.1 70.6 %copy-start.14 = (f32[256,8]{1,0:T(8,128)S(1)}, f32[256,8]{1,0:T(8,128)}, u32[]{:S(2)}) copy-start(f32[256,8]{1,0:T(8,128)} %broadcast_subtract_fusion.valid_ref) | copy-start | bytes 24580
  127.1 70.6 %copy-start.26 = (f32[256,256]{1,0:T(8,128)S(1)}, f32[256,256]{1,0:T(8,128)}, u32[]{:S(2)}) copy-start(f32[256,256]{1,0:T(8,128)} %copy-done.25) | copy-start | bytes 786436
  127.2 70.6 %copy-start.28 = (f32[256,256]{1,0:T(8,128)S(1)}, f32[256,256]{1,0:T(8,128)}, u32[]{:S(2)}) copy-start(f32[256,256]{1,0:T(8,128)} %copy-done.27) | copy-start | bytes 786436
  127.2 70.6 %copy-start.38 = (f32[4,256]{1,0:T(4,128)S(1)}, f32[4,256]{1,0:T(4,128)}, u32[]{:S(2)}) copy-start(f32[4,256]{1,0:T(4,128)} %copy-done.37) | copy-start | bytes 12292
  127.2 70.6 %copy-start.40 = (f32[4,256]{1,0:T(4,128)S(1)}, f32[4,256]{1,0:T(4,128)}, u32[]{:S(2)}) copy-start(f32[4,256]{1,0:T(4,128)} %copy-done.39) | copy-start | bytes 12292
  157.6 55.2 %copy-start.20 = (bf16[256,2048]{1,0:T(8,128)(2,1)}, bf16[256,2048]{1,0:T(8,128)(2,1)S(1)}, u32[]{:S(2)}) copy-start(bf16[256,2048]{1,0:T(8,128)(2,1)S(1)} %get-tuple-element.72.refs_3_) | copy-start | bytes 3145732
  157.6 55.2 %copy-start.41 = (f32[16,8,256]{2,1,0:T(8,128)}, f32[16,8,256]{2,1,0:T(8,128)S(1)}, u32[]{:S(2)}) copy-start(f32[16,8,256]{2,1,0:T(8,128)S(1)} %get-tuple-element.73) | copy-start | bytes 393220
  217.0 13.5 %collective-permute-start.2 = (f32[3,2560]{1,0:T(4,128)S(1)}, f32[3,2560]{1,0:T(4,128)S(1)}, u32[]{:S(2)}, u32[]{:S(2)}) collective-permute-start(f32[3,2560]{1,0:T(4,128)S(1)} %pad_maximum_fusion.1), channel_id=1, source_target_pairs={{2,0},{4,2},{6,4},{8,6},{10,8},{12,10},{14,12},{3,1},{5,3},{7,5},{... | collective-permute-start | bytes 92168 | tf_op jit(solution)/shard_map/ppermute | solution.py:249
  (41 other events, 92.9 us)

commit v3 on v2

--- a/solution.py
+++ b/solution.py
@@ -102,7 +102,7 @@
 
 def mix_kernel(
     xc, bc, cc, z, state, cols_ref, rows_ref, seg_ref, gw, skip,
-    mixed, squares, numer, scores,
+    mixed, sums, squares, numer, scores,
 ):
     k = pl.program_id(0)
 
@@ -131,6 +131,13 @@
     squares[...] += gated * gated
     numer[...] += gated * gw[...]
 
+    @pl.when(k == pl.num_programs(0) - 1)
+    def _():
+        sums[...] = pair_put(
+            jnp.sum(squares[...], axis=1, keepdims=True),
+            jnp.sum(numer[...], axis=1, keepdims=True),
+        )
+
 
 def back_kernel(
     xc, bc, cc, z, state, cols_ref, rows_ref, seg_ref, gw, skip, mixed, vcols,
@@ -157,6 +164,7 @@
     dz[...] = (dgated * m * (s * (1.0 + zz * (1.0 - s)))).astype(bf16)
     dy = dgated * gate
     dyb = dy.astype(bf16)
+    dyb_t = dy.T.astype(bf16)
     outs = []
     rowsums = []
     colsums = []
@@ -167,12 +175,12 @@
         fd = f * dt_row
         sc = scores[...]
         dm = dot(dyb[:, sl], x[:, sl], 1, 1)
-        outs.append(dot((sc * fd).astype(bf16), dyb[:, sl], 0, 0))
+        outs.append(dot(dyb_t[sl], (sc * fd).astype(bf16), 1, 0))
         dscores[...] += fd * dm
         q = sc * f * dm
         rowsums.append(jnp.sum(q * dt_row, axis=1, keepdims=True))
         colsums.append(jnp.sum(q, axis=0, keepdims=True))
-    dx[...] = jnp.concatenate(outs, axis=1) + skip[...] * dy
+    dx[...] = jnp.concatenate(outs, axis=0).T + skip[...] * dy
     reach = dy * spread(cols, 2)
     reachb = reach.astype(bf16)
     carried = dot(cc[...], state[...], 1, 1)
@@ -250,7 +258,7 @@
 
 
 MESH = pl.DeviceIdType.MESH
-CHUNKS = 4
+CHUNKS = 8
 
 
 def carry_kernel(sign, count, s_ref, mine_ref, peer_ref, out, other, came, going, sems):
@@ -397,7 +405,7 @@
 
 def move(arrays, to_heads, collective):
     count = len(arrays)
-    anywhere = pl.BlockSpec(memory_space=pl.ANY)
+    anywhere = pl.BlockSpec(memory_space=pltpu.VMEM)
     shapes = []
     for a in arrays:
         r, w = a.shape
@@ -408,7 +416,9 @@
         in_specs=[anywhere] * count,
         out_specs=[anywhere] * count,
         scratch_shapes=[pltpu.SemaphoreType.DMA((3, count))],
-        compiler_params=pltpu.CompilerParams(collective_id=collective, has_side_effects=True),
+        compiler_params=pltpu.CompilerParams(
+            collective_id=collective, has_side_effects=True, vmem_limit_bytes=32 * 1024 * 1024
+        ),
     )(*arrays)
 
 
@@ -492,7 +502,6 @@
     r8 = pl.BlockSpec((1, 8, T), lambda k: (k, 0, 0))
     st = pl.BlockSpec((PAIR, STATE), lambda k: (k, 0))
     tt = pl.BlockSpec((T, T), lambda k: (0, 0))
-    acc = pl.BlockSpec((T, PAIR), lambda k: (0, 0))
     params = pltpu.CompilerParams(
         dimension_semantics=("arbitrary",), vmem_limit_bytes=32 * 1024 * 1024
     )
@@ -514,17 +523,17 @@
 
     state = carry(add, mine_decay, peer_decay, 1)
 
-    mixed, squares, numer = pl.pallas_call(
+    mixed, sums_out = pl.pallas_call(
         mix_kernel,
         grid=(pairs,),
         in_specs=[px, pg, pg, px, st, c8, r8, tt, r1x, r1x],
-        out_specs=[px, acc, acc],
-        out_shape=[sds((T, W)), sds((T, PAIR)), sds((T, PAIR))],
-        scratch_shapes=[square],
+        out_specs=[px, v8],
+        out_shape=[sds((T, W)), sds((T, 8))],
+        scratch_shapes=[pltpu.VMEM((T, PAIR), f32), pltpu.VMEM((T, PAIR), f32), square],
         compiler_params=params,
     )(xc, bc, cc, z, state, cols, rowvals, seg, gw, skip_row)
 
-    both = lax.psum(jnp.stack([jnp.sum(squares, axis=1), jnp.sum(numer, axis=1)]), "tp")
+    both = lax.psum(sums_out[:, :2].T, "tp")
     width_all = W * tpn
     rms = jnp.sqrt(both[0] / width_all + epsilon)
     values = both[1] / rms

time: 281 us -> 202 us (0.72)
  Pallas kernels: 197 us -> 115 us
  local copies, waits for them, and re-layouts: 51.5 us -> 56.5 us
  other arithmetic: 15.8 us -> 11.4 us
    pallas_call x2, Pallas kernels: 76.4 us -> 6.18 us  [move(): pl.pallas_call(partial(move_kernel, to_heads, count), out_shape=shapes, i...]
    unnamed x148 -> x160, local copies, waits for them, and re-layouts: 26.2 us -> 35.2 us
    pallas_call x2, Pallas kernels: 57.7 us -> 48.8 us  [carry(): pl.pallas_call(partial(carry_kernel, sign, count), out_shape=jax.ShapeDty...]
    reduce_sum x2 -> x0, other arithmetic: 3.18 us -> none  [the longest x1 1.59 us: shards(): jnp.sum(squares, axis=1)]
  transfers between devices with their start and end apart: 3 -> 3, of which waited for: 0 -> 0; matrix products, arithmetic and copies ran while one was open for 7% -> 10% of each run, Pallas kernels for 4% -> 5%
where the time goes in v3:
time: 202 us; the launch traced here: 201 us
  Pallas kernels  115 us (57%)
  local copies, waits for them, and re-layouts  56.5 us (28%)
  other arithmetic  11.4 us (6%)
  starting transfers between devices  7.58 us (4%)
  blocking collectives  4.98 us (2%)
  between operations  3.51 us (2%)
    pallas_call x2, Pallas kernels, carry(): pl.pallas_call(partial(carry_kernel, sign, count), out_shape=jax.ShapeDty...  48.8 us
    unnamed x160, local copies, waits for them, and re-layouts  35.2 us
    pallas_call x1, Pallas kernels, shards(): pl.pallas_call(back_kernel, grid=(pairs,), in_specs=[px, pg, pg, px, st,...  26.5 us
    pallas_call x1, Pallas kernels, shards(): pl.pallas_call(last_kernel, grid=(pairs,), in_specs=[px, pg, st, st, c8,...  15 us
    pallas_call x1, Pallas kernels, shards(): pl.pallas_call(conv_kernel, grid=(pairs,), in_specs=[px, pg, pg, t8x, t8g...  9.74 us
    transpose x4, local copies, waits for them, and re-layouts, from_cols(): return a[:, :, :2].transpose(1, 0, 2).reshape(T, H)  9.31 us
    pallas_call x1, Pallas kernels, shards(): pl.pallas_call(mix_kernel, grid=(pairs,), in_specs=[px, pg, pg, px, st, c...  8.94 us
    pallas_call x2, Pallas kernels, move(): pl.pallas_call(partial(move_kernel, to_heads, count), out_shape=shapes, i...  6.18 us
  transfers between devices with their start and end apart: 3, of which 0 were waited for; matrix products, arithmetic and copies ran while one was open for 10% of the time, Pallas kernels for 5%

profile of v3, /device:TPU:0, one launch (start us, length us, event | category | flops | bytes accessed | tf_op | source)
XLA Modules:
  0.0 200.7 jit_solution(6555331196000554267)
XLA Ops:
  4.9 1.2 copy-done.22
  6.1 1.2 copy-done.23
  9.2 3.1 %shard_map.199 = (bf16[256,2048]{1,0:T(8,128)(2,1)S(1)}, bf16[256,256]{1,0:T(8,128)(2,1)S(1)}, bf16[256,256]{1,0:T(8,128)(2,1)S(1)}, bf16[256,2048]{1,0:T(8,128)(2,1)S(1)}, bf16[256,128]{1,0:T(8,128)(2,1)S(1)}) custom-call(bf16[128,4096]{1,0:T(8,128)(2,1)S(1)} %copy-done.22, bf16[128,512]{1,0:T(8,128)(2,1)S(1)} %copy-done.42, ...), custom_call_target="tpu_custom_call" | custom-call | tf_op jit(solution)/shard_map/pallas_call | solution.py:413
  16.4 4.8 %collective-permute-start = (bf16[3,2560]{1,0:T(4,128)(2,1)S(1)}, bf16[3,2560]{1,0:T(4,128)(2,1)S(1)}, u32[]{:S(2)}, u32[]{:S(2)}) collective-permute-start(bf16[3,2560]{1,0:T(4,128)(2,1)S(1)} %maximum_multiply_fusion), channel_id=1, source_target_pairs={{0,2},{2,4},{4,6},{6,8},{8,10},{10,12},{12,14},{1,3},{3,5},{5,7},{... | collective-permute-start | bytes 46088 | tf_op jit(solution)/shard_map/ppermute | solution.py:257
  24.2 1.5 collective-permute-start.1
  30.8 1.2 copy-done.21
  33.8 9.7 %shard_map.200 = (bf16[256,2048]{1,0:T(8,128)(2,1)S(1)}, bf16[256,256]{1,0:T(8,128)(2,1)S(1)}, bf16[256,256]{1,0:T(8,128)(2,1)S(1)}, f32[256,2048]{1,0:T(8,128)S...) custom-call(bf16[256,2048]{1,0:T(8,128)(2,1)S(1)} %copy-done.21, ...), custom_call_target="tpu_custom_call" | custom-call | tf_op jit(solution)/shard_map/pallas_call | solution.py:511
  43.6 1.3 copy-done.10
  47.2 15.8 %shard_map.201 = bf16[32,64,128]{2,1,0:T(8,128)(2,1)S(1)} custom-call(bf16[32,64,128]{2,1,0:T(8,128)(2,1)S(1)} %bitcast.66, f32[32,1,128]{2,1,0:T(1,128)S(1)} %broadcast_in_dim.69.mine_ref, f32[32,1,128]{2,1,0:T(1,128)S(1)} %broadcast_in_dim.70.peer_ref), custom_call_target="tpu_custom_call" | custom-call | tf_op jit(solution)/shard_map/pallas_call | solution.py:350
  63.0 8.9 %shard_map.202 = (f32[256,2048]{1,0:T(8,128)S(1)}, f32[256,8]{1,0:T(8,128)S(1)}) custom-call(bf16[256,2048]{1,0:T(8,128)(2,1)S(1)} %get-tuple-element.47.xc, bf16[256,256]{1,0:T(8,128)(2,1)S(1)} %get-tuple-element.48.bc, bf16[256,256]{1,0:T(8,128)(2,1)S(1)} %get-tuple-element.49.cc, bf16[256,2048]{1,0:T(8,128)(2,1)S(1)} %copy-done.5, ...), custom_call_target="tpu_custom_call" | custom-call | tf_op jit(solution)/shard_map/pallas_call | solution.py:526
  72.0 1.3 copy-done.12
  74.0 5.0 %psum.7 = f32[2,256]{0,1:T(8,128)} all-reduce(f32[2,256]{0,1:T(8,128)} %slice_bitcast_fusion.2), channel_id=1, replica_groups=mesh['group'=2,'ctx'=8,'tp'=2] {'tp'}, use_global_device_ids=true, to_apply=%region_0.1 | all-reduce | flops 512 | bytes 4096 | tf_op jit(solution)/shard_map/psum | solution.py:536
  78.9 1.7 slice_reduce_fusion.2
  80.7 1.3 fusion.27
  82.0 1.5 stack.17
  83.5 1.5 copy.129.vcols
  85.0 1.0 copy-done.2
  86.0 1.2 copy-done.6
  87.2 1.6 copy-done.13
  92.5 26.5 %shard_map.203 = (bf16[256,2048]{1,0:T(8,128)(2,1)S(1)}, f32[256,2048]{1,0:T(8,128)S(1)}, f32[256,256]{1,0:T(8,128)S(1)}, f32[256,256]{1,0:T(8,128)S(1)}, bf16[2...) custom-call(bf16[256,2048]{1,0:T(8,128)(2,1)S(1)} %get-tuple-element.47.xc, ...), custom_call_target="tpu_custom_call" | custom-call | tf_op jit(solution)/shard_map/pallas_call | solution.py:546
  119.0 1.3 copy-done.7
  120.3 33.1 %shard_map.204 = bf16[32,64,128]{2,1,0:T(8,128)(2,1)S(1)} custom-call(bf16[32,64,128]{2,1,0:T(8,128)(2,1)S(1)} %bitcast.67, f32[32,1,128]{2,1,0:T(1,128)S(1)} %broadcast_in_dim.69.mine_ref, f32[32,1,128]{2,1,0:T(1,128)S(1)} %broadcast_in_dim.70.peer_ref), custom_call_target="tpu_custom_call" | custom-call | tf_op jit(solution)/shard_map/pallas_call | solution.py:350
  153.5 15.0 %shard_map.205 = (bf16[256,2048]{1,0:T(8,128)(2,1)S(1)}, bf16[256,256]{1,0:T(8,128)(2,1)S(1)}, bf16[256,256]{1,0:T(8,128)(2,1)S(1)}, f32[8,2048]{1,0:T(8,128)S(1...) custom-call(bf16[256,2048]{1,0:T(8,128)(2,1)S(1)} %get-tuple-element, ...), custom_call_target="tpu_custom_call" | custom-call | tf_op jit(solution)/shard_map/pallas_call | solution.py:561
  168.5 1.3 copy-done.9
  174.3 1.3 collective-permute-start.2
  175.7 3.1 %slice_bitcast_fusion.1 = f32[256,16,2]{2,0,1:T(8,128)} fusion(f32[16,256,8]{2,1,0:T(8,128)} %copy-done.9), kind=kLoop, calls=%fused_computation.1 | loop fusion | bytes 65536 | tf_op jit(solution)/shard_map/transpose | solution.py:576
  178.8 2.4 %copy.132 = f32[256,16,2]{0,2,1:T(2,128)S(1)} copy(f32[256,16,2]{2,0,1:T(8,128)} %slice_bitcast_fusion.1) | data formatting | bytes 65536 | tf_op jit(solution)/shard_map/transpose | solution.py:576
  181.9 1.5 slice_bitcast_fusion
  183.4 2.4 %copy.134 = f32[256,16,2]{0,2,1:T(2,128)S(1)} copy(f32[256,16,2]{2,0,1:T(8,128)} %slice_bitcast_fusion) | data formatting | bytes 65536 | tf_op jit(solution)/shard_map/transpose | solution.py:576
  186.6 1.2 fusion.3
  189.9 3.1 %shard_map.206 = (bf16[128,4096]{1,0:T(8,128)(2,1)S(1)}, bf16[128,512]{1,0:T(8,128)(2,1)S(1)}, bf16[128,512]{1,0:T(8,128)(2,1)S(1)}, bf16[128,4096]{1,0:T(8,128)(2,1)S(1)}, bf16[128,256]{1,0:T(8,128)(2,1)S(1)}) custom-call(bf16[256,2048]{1,0:T(8,128)(2,1)S(1)} %dynamic_update_slice.9.refs_0_, bf16[256,256]{1,0:T(8,128)(2,1)S(1)} %dynamic_update_slice.10.refs_1_, ...), custom_call_target="tpu_custom_call" | custom-call | tf_op jit(solution)/shard_map/pallas_call | solution.py:413
  196.1 2.3 %copy.151 = bf16[128,4096]{1,0:T(8,128)(2,1)} copy(bf16[128,4096]{1,0:T(8,128)(2,1)} %copy-done.28) | data formatting | bytes 2097152
  (228 shorter events, 37.9 us)
Async XLA Ops:
  0.6 27.4 %copy-start = (f32[4,4096]{1,0:T(4,128)S(1)}, f32[4,4096]{1,0:T(4,128)}, u32[]{:S(2)}) copy-start(f32[4,4096]{1,0:T(4,128)} %param.21) | copy-start | bytes 196612
  0.6 20.5 %copy-start.73 = (f32[64]{0:T(128)S(1)}, f32[64]{0:T(128)}, u32[]{:S(2)}) copy-start(f32[64]{0:T(128)} %param.25) | copy-start | bytes 772
  0.7 20.6 %copy-start.74 = (f32[64]{0:T(128)S(1)}, f32[64]{0:T(128)}, u32[]{:S(2)}) copy-start(f32[64]{0:T(128)} %param.24) | copy-start | bytes 772
  9.2 16.6 %copy-start.66 = (s32[256]{0:T(256)S(1)}, s32[256]{0:T(256)}, u32[]{:S(2)}) copy-start(s32[256]{0:T(256)} %param.29) | copy-start | bytes 3076
  13.3 15.9 %copy-start.36 = (bf16[256,128]{1,0:T(8,128)(2,1)}, bf16[256,128]{1,0:T(8,128)(2,1)S(1)}, u32[]{:S(2)}) copy-start(bf16[256,128]{1,0:T(8,128)(2,1)S(1)} %get-tuple-element.46) | copy-start | bytes 196612
  13.3 14.0 %copy-start.70 = (f32[256]{0:T(256)S(1)}, f32[256]{0:T(256)}, u32[]{:S(2)}) copy-start(f32[256]{0:T(256)} %param.31) | copy-start | bytes 3076
  13.3 14.0 %copy-start.71 = (s32[256]{0:T(256)S(1)}, s32[256]{0:T(256)}, u32[]{:S(2)}) copy-start(s32[256]{0:T(256)} %param.30) | copy-start | bytes 3076
  13.3 14.8 %copy-start.64 = (f32[4096]{0:T(1024)S(1)}, f32[4096]{0:T(1024)}, u32[]{:S(2)}) copy-start(f32[4096]{0:T(1024)} %param.28) | copy-start | bytes 49156
  13.3 14.8 %copy-start.65 = (f32[4096]{0:T(1024)S(1)}, f32[4096]{0:T(1024)}, u32[]{:S(2)}) copy-start(f32[4096]{0:T(1024)} %param.27) | copy-start | bytes 49156
  13.3 15.6 %copy-start.67 = (f32[4,512]{1,0:T(4,128)S(1)}, f32[4,512]{1,0:T(4,128)}, u32[]{:S(2)}) copy-start(f32[4,512]{1,0:T(4,128)} %param.23) | copy-start | bytes 24580
  13.3 15.6 %copy-start.68 = (f32[4,512]{1,0:T(4,128)S(1)}, f32[4,512]{1,0:T(4,128)}, u32[]{:S(2)}) copy-start(f32[4,512]{1,0:T(4,128)} %param.22) | copy-start | bytes 24580
  13.3 15.6 %copy-start.75 = (f32[64]{0:T(128)S(1)}, f32[64]{0:T(128)}, u32[]{:S(2)}) copy-start(f32[64]{0:T(128)} %param.26) | copy-start | bytes 772
  16.4 13.5 %collective-permute-start = (bf16[3,2560]{1,0:T(4,128)(2,1)S(1)}, bf16[3,2560]{1,0:T(4,128)(2,1)S(1)}, u32[]{:S(2)}, u32[]{:S(2)}) collective-permute-start(bf16[3,2560]{1,0:T(4,128)(2,1)S(1)} %maximum_multiply_fusion), channel_id=1, source_target_pairs={{0,2},{2,4},{4,6},{6,8},{8,10},{10,12},{12,14},{1,3},{3,5},{5,7},{... | collective-permute-start | bytes 46088 | tf_op jit(solution)/shard_map/ppermute | solution.py:257
  24.2 21.5 %collective-permute-start.1 = (f32[32]{0:T(128)}, f32[32]{0:T(128)}, u32[]{:S(2)}, u32[]{:S(2)}) collective-permute-start(f32[32]{0:T(128)} %slice_bitcast_fusion.3), channel_id=1, source_target_pairs={{0,2},{2,0},{4,6},{6,4},{8,10},{10,8},{12,14},{14,12},{1,3},{3,1},... | collective-permute-start | bytes 392 | tf_op jit(solution)/shard_map/ppermute | solution.py:477
  28.9 14.7 %copy-start.52 = (f32[4,256]{1,0:T(4,128)}, f32[4,256]{1,0:T(4,128)S(1)}, u32[]{:S(2)}) copy-start(f32[4,256]{1,0:T(4,128)S(1)} %get-tuple-element.138.wc) | copy-start | bytes 12292
  28.9 14.7 %copy-start.54 = (f32[4,256]{1,0:T(4,128)}, f32[4,256]{1,0:T(4,128)S(1)}, u32[]{:S(2)}) copy-start(f32[4,256]{1,0:T(4,128)S(1)} %get-tuple-element.139.wb) | copy-start | bytes 12292
  33.8 29.1 %copy-start.5 = (bf16[256,2048]{1,0:T(8,128)(2,1)S(1)}, bf16[256,2048]{1,0:T(8,128)(2,1)}, u32[]{:S(2)}) copy-start(bf16[256,2048]{1,0:T(8,128)(2,1)} %copy-done.4) | copy-start | bytes 3145732
  33.8 29.2 %copy-start.18 = (f32[16,8,256]{2,1,0:T(8,128)S(1)}, f32[16,8,256]{2,1,0:T(8,128)}, u32[]{:S(2)}) copy-start(f32[16,8,256]{2,1,0:T(8,128)} %maximum_maximum_fusion.rows_ref) | copy-start | bytes 393220
  45.7 17.3 %copy-start.34 = (f32[256,256]{1,0:T(8,128)}, f32[256,256]{1,0:T(8,128)S(1)}, u32[]{:S(2)}) copy-start(f32[256,256]{1,0:T(8,128)S(1)} %get-tuple-element.60.uc) | copy-start | bytes 786436
  45.7 26.3 %copy-start.16 = (bf16[256,256]{1,0:T(8,128)(2,1)}, bf16[256,256]{1,0:T(8,128)(2,1)S(1)}, u32[]{:S(2)}) copy-start(bf16[256,256]{1,0:T(8,128)(2,1)S(1)} %get-tuple-element.48.bc) | copy-start | bytes 393220
  45.7 26.3 %copy-start.30 = (bf16[256,256]{1,0:T(8,128)(2,1)}, bf16[256,256]{1,0:T(8,128)(2,1)S(1)}, u32[]{:S(2)}) copy-start(bf16[256,256]{1,0:T(8,128)(2,1)S(1)} %get-tuple-element.49.cc) | copy-start | bytes 393220
  63.0 9.0 %copy-start.1 = (bf16[32,64,128]{2,1,0:T(8,128)(2,1)}, bf16[32,64,128]{2,1,0:T(8,128)(2,1)S(1)}, u32[]{:S(2)}) copy-start(bf16[32,64,128]{2,1,0:T(8,128)(2,1)S(1)} %shard_map.201) | copy-start | bytes 1572868
  92.5 60.9 %copy-start.3 = (bf16[32,64,128]{2,1,0:T(8,128)(2,1)S(1)}, bf16[32,64,128]{2,1,0:T(8,128)(2,1)}, u32[]{:S(2)}) copy-start(bf16[32,64,128]{2,1,0:T(8,128)(2,1)} %copy-done.1) | copy-start | bytes 1572868
  92.5 60.9 %copy-start.11 = (f32[256,2048]{1,0:T(8,128)S(1)}, f32[256,2048]{1,0:T(8,128)}, u32[]{:S(2)}) copy-start(f32[256,2048]{1,0:T(8,128)} %copy-done.10) | copy-start | bytes 6291460
  92.5 61.0 %copy-start.15 = (f32[256,8]{1,0:T(8,128)S(1)}, f32[256,8]{1,0:T(8,128)}, u32[]{:S(2)}) copy-start(f32[256,8]{1,0:T(8,128)} %broadcast_subtract_fusion.valid_ref) | copy-start | bytes 24580
  92.5 61.0 %copy-start.33 = (f32[256,256]{1,0:T(8,128)S(1)}, f32[256,256]{1,0:T(8,128)}, u32[]{:S(2)}) copy-start(f32[256,256]{1,0:T(8,128)} %copy-done.32) | copy-start | bytes 786436
  92.5 61.0 %copy-start.35 = (f32[256,256]{1,0:T(8,128)S(1)}, f32[256,256]{1,0:T(8,128)}, u32[]{:S(2)}) copy-start(f32[256,256]{1,0:T(8,128)} %copy-done.34) | copy-start | bytes 786436
  92.5 61.0 %copy-start.53 = (f32[4,256]{1,0:T(4,128)S(1)}, f32[4,256]{1,0:T(4,128)}, u32[]{:S(2)}) copy-start(f32[4,256]{1,0:T(4,128)} %copy-done.52) | copy-start | bytes 12292
  92.5 61.0 %copy-start.55 = (f32[4,256]{1,0:T(4,128)S(1)}, f32[4,256]{1,0:T(4,128)}, u32[]{:S(2)}) copy-start(f32[4,256]{1,0:T(4,128)} %copy-done.54) | copy-start | bytes 12292
  120.3 48.1 %copy-start.24 = (bf16[256,2048]{1,0:T(8,128)(2,1)}, bf16[256,2048]{1,0:T(8,128)(2,1)S(1)}, u32[]{:S(2)}) copy-start(bf16[256,2048]{1,0:T(8,128)(2,1)S(1)} %get-tuple-element.70.refs_3_) | copy-start | bytes 3145732
  120.3 48.1 %copy-start.56 = (f32[16,8,256]{2,1,0:T(8,128)}, f32[16,8,256]{2,1,0:T(8,128)S(1)}, u32[]{:S(2)}) copy-start(f32[16,8,256]{2,1,0:T(8,128)S(1)} %get-tuple-element.71) | copy-start | bytes 393220
  174.3 14.2 %collective-permute-start.2 = (f32[3,2560]{1,0:T(4,128)}, f32[3,2560]{1,0:T(4,128)}, u32[]{:S(2)}, u32[]{:S(2)}) collective-permute-start(f32[3,2560]{1,0:T(4,128)} %pad_maximum_fusion.1), channel_id=1, source_target_pairs={{2,0},{4,2},{6,4},{8,6},{10,8},{12,10},{14,12},{3,1},{5,3},{7,5},{... | collective-permute-start | bytes 92168 | tf_op jit(solution)/shard_map/ppermute | solution.py:257
  (47 other events, 109.4 us)

commit v4 on v3

--- a/solution.py
+++ b/solution.py
@@ -68,6 +68,12 @@
     for i, c in enumerate(cols):
         out = jnp.where(lane == i, c, out)
     return out
+
+
+def lane_put(out, k, a, b):
+    lane = lax.broadcasted_iota(jnp.int32, out.shape, 1)
+    kept = out[...]
+    out[...] = jnp.where(lane == 2 * k, a, jnp.where(lane == 2 * k + 1, b, kept))
 
 
 def conv_kernel(
@@ -190,7 +196,12 @@
         rowsums[j] = rowsums[j] + jnp.sum(both[:, sl], axis=1, keepdims=True)
     dcacc[...] += dot(reachb, state[...], 1, 0)
     ds[...] = dot(reachb, cc[...], 0, 0).astype(bf16)
-    colout[0] = pair_put(*rowsums)
+
+    @pl.when(k == 0)
+    def _():
+        colout[...] = jnp.zeros(colout.shape, f32)
+
+    lane_put(colout, k, rowsums[0], rowsums[1])
     sub = lax.broadcasted_iota(jnp.int32, (8, colsums[0].shape[1]), 0)
     rowout[0] = jnp.where(sub == 0, colsums[0], jnp.where(sub == 1, colsums[1], 0.0))
 
@@ -227,7 +238,13 @@
     g = gstate[...]
     gbx = dot(bc[...], g, 1, 1)
     xg = x * gbx
-    stats[0] = pair_put(
+
+    @pl.when(k == 0)
+    def _():
+        stats[...] = jnp.zeros(stats.shape, f32)
+
+    lane_put(
+        stats, k,
         jnp.sum(xg[:, :HEAD_DIM], axis=1, keepdims=True),
         jnp.sum(xg[:, HEAD_DIM:], axis=1, keepdims=True),
     )
@@ -502,6 +519,8 @@
     r8 = pl.BlockSpec((1, 8, T), lambda k: (k, 0, 0))
     st = pl.BlockSpec((PAIR, STATE), lambda k: (k, 0))
     tt = pl.BlockSpec((T, T), lambda k: (0, 0))
+    lane_width = -(-H // 128) * 128
+    wide = pl.BlockSpec((T, lane_width), lambda k: (0, 0))
     params = pltpu.CompilerParams(
         dimension_semantics=("arbitrary",), vmem_limit_bytes=32 * 1024 * 1024
     )
@@ -547,10 +566,10 @@
         back_kernel,
         grid=(pairs,),
         in_specs=[px, pg, pg, px, st, c8, r8, tt, r1x, r1x, px, v8],
-        out_specs=[px, px, pg, pg, st, c8, r8],
+        out_specs=[px, px, pg, pg, st, wide, r8],
         out_shape=[
             sds((T, W), bf16), sds((T, W)), sds((T, N)), sds((T, N)), sds((W, STATE), bf16),
-            sds((pairs, T, 8)), sds((pairs, 8, T)),
+            sds((T, lane_width)), sds((pairs, 8, T)),
         ],
         scratch_shapes=[square, square, pltpu.VMEM((T, STATE), f32)],
         compiler_params=params,
@@ -562,22 +581,19 @@
         last_kernel,
         grid=(pairs,),
         in_specs=[px, pg, st, st, c8, px, pg, pg, px, pg, pg, w4x, w4g, w4g, v8],
-        out_specs=[px, pg, pg, t8x, t8g, t8g, t8x, t8g, t8g, c8, r8s(STATE)],
+        out_specs=[px, pg, pg, t8x, t8g, t8g, t8x, t8g, t8g, wide, r8s(STATE)],
         out_shape=[
             sds((T, W), bf16), sds((T, N), bf16), sds((T, N), bf16),
             sds((8, W)), sds((8, N)), sds((8, N)), sds((8, W)), sds((8, N)), sds((8, N)),
-            sds((pairs, T, 8)), sds((pairs, 8, STATE)),
+            sds((T, lane_width)), sds((pairs, 8, STATE)),
         ],
         scratch_shapes=[pltpu.VMEM((T, STATE), f32), ext],
         compiler_params=params,
     )(xc, bc, gstate, state, cols, dx, dcg, dbg, ux, ub, uc, wx, wb, wc, valid)
 
-    def from_cols(a):
-        return a[:, :, :2].transpose(1, 0, 2).reshape(T, H)
-
-    row_part = from_cols(colout)
+    row_part = colout[:, :H]
     col_sum = rowout[:, :2, :].reshape(H, T).T
-    xg = from_cols(stats)
+    xg = stats[:, :H]
     ginner = jnp.sum(inner[:, :2, :], axis=2).reshape(H)
     tail_part = we * xg
     dcum = row_part - dt * col_sum - tail_part

time: 202 us -> 191 us (0.946)
  local copies, waits for them, and re-layouts: 56.5 us -> 45.5 us
    transpose x4 -> x0, local copies, waits for them, and re-layouts: 9.31 us -> none  [from_cols(): return a[:, :, :2].transpose(1, 0, 2).reshape(T, H)]
    pallas_call x1, Pallas kernels: 15 us -> 12.7 us  [shards(): pl.pallas_call(last_kernel, grid=(pairs,), in_specs=[px, pg, st, st, c8,...]
    unnamed x160 -> x162, local copies, waits for them, and re-layouts: 35.2 us -> 34.3 us
  transfers between devices with their start and end apart: 3 -> 3, of which waited for: 0 -> 1; matrix products, arithmetic and copies ran while one was open for 10% -> 5% of each run, Pallas kernels for 5% -> 5%
where the time goes in v4:
time: 191 us; the launch traced here: 190 us
  Pallas kernels  113 us (59%)
  local copies, waits for them, and re-layouts  45.5 us (24%)
  other arithmetic  11.4 us (6%)
  starting transfers between devices  7.59 us (4%)
  blocking collectives  4.98 us (3%)
  between operations  3.5 us (2%)
  matrix products  2.02 us (1%)
    pallas_call x2, Pallas kernels, carry(): pl.pallas_call(partial(carry_kernel, sign, count), out_shape=jax.ShapeDty...  48.9 us
    unnamed x162, local copies, waits for them, and re-layouts  34.3 us
    pallas_call x1, Pallas kernels, shards(): pl.pallas_call(back_kernel, grid=(pairs,), in_specs=[px, pg, pg, px, st,...  26.7 us
    pallas_call x1, Pallas kernels, shards(): pl.pallas_call(last_kernel, grid=(pairs,), in_specs=[px, pg, st, st, c8,...  12.7 us
    pallas_call x1, Pallas kernels, shards(): pl.pallas_call(conv_kernel, grid=(pairs,), in_specs=[px, pg, pg, t8x, t8g...  9.74 us
    pallas_call x1, Pallas kernels, shards(): pl.pallas_call(mix_kernel, grid=(pairs,), in_specs=[px, pg, pg, px, st, c...  8.94 us
    pallas_call x2, Pallas kernels, move(): pl.pallas_call(partial(move_kernel, to_heads, count), out_shape=shapes, i...  6.18 us
    ppermute x2, starting transfers between devices, hop(): lax.ppermute(value, 'ctx', [(i, i + steps) for i in range(initial, last)])  6.07 us
  transfers between devices with their start and end apart: 3, of which 1 were waited for; matrix products, arithmetic and copies ran while one was open for 5% of the time, Pallas kernels for 5%

profile of v4, /device:TPU:0, one launch (start us, length us, event | category | flops | bytes accessed | tf_op | source)
XLA Modules:
  0.0 189.5 jit_solution(13803712458363780569)
XLA Ops:
  4.9 1.2 copy-done.19
  6.1 1.2 copy-done.20
  9.2 3.1 %shard_map.199 = (bf16[256,2048]{1,0:T(8,128)(2,1)S(1)}, bf16[256,256]{1,0:T(8,128)(2,1)S(1)}, bf16[256,256]{1,0:T(8,128)(2,1)S(1)}, bf16[256,2048]{1,0:T(8,128)(2,1)S(1)}, bf16[256,128]{1,0:T(8,128)(2,1)S(1)}) custom-call(bf16[128,4096]{1,0:T(8,128)(2,1)S(1)} %copy-done.19, bf16[128,512]{1,0:T(8,128)(2,1)S(1)} %copy-done.39, ...), custom_call_target="tpu_custom_call" | custom-call | tf_op jit(solution)/shard_map/pallas_call | solution.py:430
  12.3 1.0 copy-done.4
  16.4 4.8 %collective-permute-start = (bf16[3,2560]{1,0:T(4,128)(2,1)S(1)}, bf16[3,2560]{1,0:T(4,128)(2,1)S(1)}, u32[]{:S(2)}, u32[]{:S(2)}) collective-permute-start(bf16[3,2560]{1,0:T(4,128)(2,1)S(1)} %maximum_multiply_fusion), channel_id=1, source_target_pairs={{0,2},{2,4},{4,6},{6,8},{8,10},{10,12},{12,14},{1,3},{3,5},{5,7},{... | collective-permute-start | bytes 46088 | tf_op jit(solution)/shard_map/ppermute | solution.py:274
  24.2 1.5 collective-permute-start.1
  30.8 1.2 copy-done.18
  33.8 9.7 %shard_map.200 = (bf16[256,2048]{1,0:T(8,128)(2,1)S(1)}, bf16[256,256]{1,0:T(8,128)(2,1)S(1)}, bf16[256,256]{1,0:T(8,128)(2,1)S(1)}, f32[256,2048]{1,0:T(8,128)S...) custom-call(bf16[256,2048]{1,0:T(8,128)(2,1)S(1)} %copy-done.18, ...), custom_call_target="tpu_custom_call" | custom-call | tf_op jit(solution)/shard_map/pallas_call | solution.py:530
  43.6 1.3 copy-done.7
  47.1 15.8 %shard_map.201 = bf16[32,64,128]{2,1,0:T(8,128)(2,1)S(1)} custom-call(bf16[32,64,128]{2,1,0:T(8,128)(2,1)S(1)} %bitcast.58, f32[32,1,128]{2,1,0:T(1,128)S(1)} %broadcast_in_dim.69.mine_ref, f32[32,1,128]{2,1,0:T(1,128)S(1)} %broadcast_in_dim.70.peer_ref), custom_call_target="tpu_custom_call" | custom-call | tf_op jit(solution)/shard_map/pallas_call | solution.py:367
  62.9 8.9 %shard_map.202 = (f32[256,2048]{1,0:T(8,128)S(1)}, f32[256,8]{1,0:T(8,128)S(1)}) custom-call(bf16[256,2048]{1,0:T(8,128)(2,1)S(1)} %get-tuple-element.47.xc, bf16[256,256]{1,0:T(8,128)(2,1)S(1)} %get-tuple-element.48.bc, bf16[256,256]{1,0:T(8,128)(2,1)S(1)} %get-tuple-element.49.cc, bf16[256,2048]{1,0:T(8,128)(2,1)S(1)} %copy-done.5, ...), custom_call_target="tpu_custom_call" | custom-call | tf_op jit(solution)/shard_map/pallas_call | solution.py:545
  71.8 1.3 copy-done.9
  73.8 5.0 %psum.7 = f32[2,256]{0,1:T(8,128)} all-reduce(f32[2,256]{0,1:T(8,128)} %slice_bitcast_fusion), channel_id=1, replica_groups=mesh['group'=2,'ctx'=8,'tp'=2] {'tp'}, use_global_device_ids=true, to_apply=%region_0.1 | all-reduce | flops 512 | bytes 4096 | tf_op jit(solution)/shard_map/psum | solution.py:555
  78.8 1.7 slice_reduce_fusion.2
  80.6 1.3 fusion.28
  81.8 1.5 stack.17
  83.4 1.5 copy.112.vcols
  84.9 1.0 copy-done.2
  85.9 1.2 copy-done.6
  87.1 1.6 copy-done.10
  92.4 26.7 %shard_map.203 = (bf16[256,2048]{1,0:T(8,128)(2,1)S(1)}, f32[256,2048]{1,0:T(8,128)S(1)}, f32[256,256]{1,0:T(8,128)S(1)}, f32[256,256]{1,0:T(8,128)S(1)}, bf16[2...) custom-call(bf16[256,2048]{1,0:T(8,128)(2,1)S(1)} %get-tuple-element.47.xc, ...), custom_call_target="tpu_custom_call" | custom-call | tf_op jit(solution)/shard_map/pallas_call | solution.py:565
  119.1 33.1 %shard_map.204 = bf16[32,64,128]{2,1,0:T(8,128)(2,1)S(1)} custom-call(bf16[32,64,128]{2,1,0:T(8,128)(2,1)S(1)} %bitcast.59, f32[32,1,128]{2,1,0:T(1,128)S(1)} %broadcast_in_dim.69.mine_ref, f32[32,1,128]{2,1,0:T(1,128)S(1)} %broadcast_in_dim.70.peer_ref), custom_call_target="tpu_custom_call" | custom-call | tf_op jit(solution)/shard_map/pallas_call | solution.py:367
  152.3 12.7 %shard_map.205 = (bf16[256,2048]{1,0:T(8,128)(2,1)S(1)}, bf16[256,256]{1,0:T(8,128)(2,1)S(1)}, bf16[256,256]{1,0:T(8,128)(2,1)S(1)}, f32[8,2048]{1,0:T(8,128)S(1...) custom-call(bf16[256,2048]{1,0:T(8,128)(2,1)S(1)} %get-tuple-element, ...), custom_call_target="tpu_custom_call" | custom-call | tf_op jit(solution)/shard_map/pallas_call | solution.py:580
  165.1 1.0 copy-done.23
  169.1 1.1 fusion.22
  172.3 1.3 collective-permute-start.2
  174.4 1.7 fusion.3
  176.7 1.5 collective-permute-done.2
  178.8 3.1 %shard_map.206 = (bf16[128,4096]{1,0:T(8,128)(2,1)S(1)}, bf16[128,512]{1,0:T(8,128)(2,1)S(1)}, bf16[128,512]{1,0:T(8,128)(2,1)S(1)}, bf16[128,4096]{1,0:T(8,128)(2,1)S(1)}, bf16[128,256]{1,0:T(8,128)(2,1)S(1)}) custom-call(bf16[256,2048]{1,0:T(8,128)(2,1)S(1)} %dynamic_update_slice.9.refs_0_, bf16[256,256]{1,0:T(8,128)(2,1)S(1)} %dynamic_update_slice.10.refs_1_, ...), custom_call_target="tpu_custom_call" | custom-call | tf_op jit(solution)/shard_map/pallas_call | solution.py:430
  181.9 1.0 copy-done.25
  185.0 2.3 %copy.129 = bf16[128,4096]{1,0:T(8,128)(2,1)} copy(bf16[128,4096]{1,0:T(8,128)(2,1)} %copy-done.25) | data formatting | bytes 2097152
  188.6 1.0 copy.132
  (222 shorter events, 33.8 us)
Async XLA Ops:
  0.6 27.4 %copy-start = (f32[4,4096]{1,0:T(4,128)S(1)}, f32[4,4096]{1,0:T(4,128)}, u32[]{:S(2)}) copy-start(f32[4,4096]{1,0:T(4,128)} %param.21) | copy-start | bytes 196612
  0.6 20.5 %copy-start.74 = (f32[64]{0:T(128)S(1)}, f32[64]{0:T(128)}, u32[]{:S(2)}) copy-start(f32[64]{0:T(128)} %param.25) | copy-start | bytes 772
  0.7 20.6 %copy-start.75 = (f32[64]{0:T(128)S(1)}, f32[64]{0:T(128)}, u32[]{:S(2)}) copy-start(f32[64]{0:T(128)} %param.24) | copy-start | bytes 772
  9.2 16.6 %copy-start.66 = (s32[256]{0:T(256)S(1)}, s32[256]{0:T(256)}, u32[]{:S(2)}) copy-start(s32[256]{0:T(256)} %param.29) | copy-start | bytes 3076
  13.3 15.8 %copy-start.33 = (bf16[256,128]{1,0:T(8,128)(2,1)}, bf16[256,128]{1,0:T(8,128)(2,1)S(1)}, u32[]{:S(2)}) copy-start(bf16[256,128]{1,0:T(8,128)(2,1)S(1)} %get-tuple-element.46) | copy-start | bytes 196612
  13.3 14.7 %copy-start.64 = (f32[4096]{0:T(1024)S(1)}, f32[4096]{0:T(1024)}, u32[]{:S(2)}) copy-start(f32[4096]{0:T(1024)} %param.28) | copy-start | bytes 49156
  13.3 14.7 %copy-start.65 = (f32[4096]{0:T(1024)S(1)}, f32[4096]{0:T(1024)}, u32[]{:S(2)}) copy-start(f32[4096]{0:T(1024)} %param.27) | copy-start | bytes 49156
  13.3 15.6 %copy-start.68 = (f32[4,512]{1,0:T(4,128)S(1)}, f32[4,512]{1,0:T(4,128)}, u32[]{:S(2)}) copy-start(f32[4,512]{1,0:T(4,128)} %param.23) | copy-start | bytes 24580
  13.3 15.6 %copy-start.69 = (f32[4,512]{1,0:T(4,128)S(1)}, f32[4,512]{1,0:T(4,128)}, u32[]{:S(2)}) copy-start(f32[4,512]{1,0:T(4,128)} %param.22) | copy-start | bytes 24580
  13.3 15.6 %copy-start.76 = (f32[64]{0:T(128)S(1)}, f32[64]{0:T(128)}, u32[]{:S(2)}) copy-start(f32[64]{0:T(128)} %param.26) | copy-start | bytes 772
  16.4 13.4 %collective-permute-start = (bf16[3,2560]{1,0:T(4,128)(2,1)S(1)}, bf16[3,2560]{1,0:T(4,128)(2,1)S(1)}, u32[]{:S(2)}, u32[]{:S(2)}) collective-permute-start(bf16[3,2560]{1,0:T(4,128)(2,1)S(1)} %maximum_multiply_fusion), channel_id=1, source_target_pairs={{0,2},{2,4},{4,6},{6,8},{8,10},{10,12},{12,14},{1,3},{3,5},{5,7},{... | collective-permute-start | bytes 46088 | tf_op jit(solution)/shard_map/ppermute | solution.py:274
  24.2 21.4 %collective-permute-start.1 = (f32[32]{0:T(128)}, f32[32]{0:T(128)}, u32[]{:S(2)}, u32[]{:S(2)}) collective-permute-start(f32[32]{0:T(128)} %slice_bitcast_fusion.1), channel_id=1, source_target_pairs={{0,2},{2,0},{4,6},{6,4},{8,10},{10,8},{12,14},{14,12},{1,3},{3,1},... | collective-permute-start | bytes 392 | tf_op jit(solution)/shard_map/ppermute | solution.py:494
  28.9 14.7 %copy-start.50 = (f32[4,256]{1,0:T(4,128)}, f32[4,256]{1,0:T(4,128)S(1)}, u32[]{:S(2)}) copy-start(f32[4,256]{1,0:T(4,128)S(1)} %get-tuple-element.138.wc) | copy-start | bytes 12292
  28.9 14.7 %copy-start.52 = (f32[4,256]{1,0:T(4,128)}, f32[4,256]{1,0:T(4,128)S(1)}, u32[]{:S(2)}) copy-start(f32[4,256]{1,0:T(4,128)S(1)} %get-tuple-element.139.wb) | copy-start | bytes 12292
  33.8 29.0 %copy-start.5 = (bf16[256,2048]{1,0:T(8,128)(2,1)S(1)}, bf16[256,2048]{1,0:T(8,128)(2,1)}, u32[]{:S(2)}) copy-start(bf16[256,2048]{1,0:T(8,128)(2,1)} %copy-done.4) | copy-start | bytes 3145732
  33.8 29.1 %copy-start.15 = (f32[16,8,256]{2,1,0:T(8,128)S(1)}, f32[16,8,256]{2,1,0:T(8,128)}, u32[]{:S(2)}) copy-start(f32[16,8,256]{2,1,0:T(8,128)} %maximum_maximum_fusion.rows_ref) | copy-start | bytes 393220
  45.6 17.2 %copy-start.31 = (f32[256,256]{1,0:T(8,128)}, f32[256,256]{1,0:T(8,128)S(1)}, u32[]{:S(2)}) copy-start(f32[256,256]{1,0:T(8,128)S(1)} %get-tuple-element.60.uc) | copy-start | bytes 786436
  45.6 26.2 %copy-start.13 = (bf16[256,256]{1,0:T(8,128)(2,1)}, bf16[256,256]{1,0:T(8,128)(2,1)S(1)}, u32[]{:S(2)}) copy-start(bf16[256,256]{1,0:T(8,128)(2,1)S(1)} %get-tuple-element.48.bc) | copy-start | bytes 393220
  45.6 26.2 %copy-start.27 = (bf16[256,256]{1,0:T(8,128)(2,1)}, bf16[256,256]{1,0:T(8,128)(2,1)S(1)}, u32[]{:S(2)}) copy-start(bf16[256,256]{1,0:T(8,128)(2,1)S(1)} %get-tuple-element.49.cc) | copy-start | bytes 393220
  92.4 59.9 %copy-start.3 = (bf16[32,64,128]{2,1,0:T(8,128)(2,1)S(1)}, bf16[32,64,128]{2,1,0:T(8,128)(2,1)}, u32[]{:S(2)}) copy-start(bf16[32,64,128]{2,1,0:T(8,128)(2,1)} %copy-done.1) | copy-start | bytes 1572868
  92.4 59.9 %copy-start.8 = (f32[256,2048]{1,0:T(8,128)S(1)}, f32[256,2048]{1,0:T(8,128)}, u32[]{:S(2)}) copy-start(f32[256,2048]{1,0:T(8,128)} %copy-done.7) | copy-start | bytes 6291460
  92.4 59.9 %copy-start.12 = (f32[256,8]{1,0:T(8,128)S(1)}, f32[256,8]{1,0:T(8,128)}, u32[]{:S(2)}) copy-start(f32[256,8]{1,0:T(8,128)} %broadcast_subtract_fusion.valid_ref) | copy-start | bytes 24580
  92.4 59.9 %copy-start.30 = (f32[256,256]{1,0:T(8,128)S(1)}, f32[256,256]{1,0:T(8,128)}, u32[]{:S(2)}) copy-start(f32[256,256]{1,0:T(8,128)} %copy-done.29) | copy-start | bytes 786436
  92.4 59.9 %copy-start.32 = (f32[256,256]{1,0:T(8,128)S(1)}, f32[256,256]{1,0:T(8,128)}, u32[]{:S(2)}) copy-start(f32[256,256]{1,0:T(8,128)} %copy-done.31) | copy-start | bytes 786436
  92.4 59.9 %copy-start.51 = (f32[4,256]{1,0:T(4,128)S(1)}, f32[4,256]{1,0:T(4,128)}, u32[]{:S(2)}) copy-start(f32[4,256]{1,0:T(4,128)} %copy-done.50) | copy-start | bytes 12292
  92.4 59.9 %copy-start.53 = (f32[4,256]{1,0:T(4,128)S(1)}, f32[4,256]{1,0:T(4,128)}, u32[]{:S(2)}) copy-start(f32[4,256]{1,0:T(4,128)} %copy-done.52) | copy-start | bytes 12292
  119.1 46.0 %copy-start.21 = (bf16[256,2048]{1,0:T(8,128)(2,1)}, bf16[256,2048]{1,0:T(8,128)(2,1)S(1)}, u32[]{:S(2)}) copy-start(bf16[256,2048]{1,0:T(8,128)(2,1)S(1)} %get-tuple-element.70.refs_3_) | copy-start | bytes 3145732
  119.1 45.9 %copy-start.54 = (f32[16,8,256]{2,1,0:T(8,128)}, f32[16,8,256]{2,1,0:T(8,128)S(1)}, u32[]{:S(2)}) copy-start(f32[16,8,256]{2,1,0:T(8,128)S(1)} %get-tuple-element.71) | copy-start | bytes 393220
  119.1 45.9 %copy-start.57 = (f32[256,128]{1,0:T(8,128)}, f32[256,128]{1,0:T(8,128)S(1)}, u32[]{:S(2)}) copy-start(f32[256,128]{1,0:T(8,128)S(1)} %get-tuple-element.73) | copy-start | bytes 393220
  152.3 16.8 %copy-start.59 = (f32[256,32]{1,0:T(8,128)S(1)}, f32[256,32]{1,0:T(8,128)}, u32[]{:S(2)}) copy-start(f32[256,32]{1,0:T(8,128)} %copy-done.58) | copy-start | bytes 98308
  152.3 22.0 %copy-start.34 = (bf16[256,128]{1,0:T(8,128)(2,1)S(1)}, bf16[256,128]{1,0:T(8,128)(2,1)}, u32[]{:S(2)}) copy-start(bf16[256,128]{1,0:T(8,128)(2,1)} %copy-done.33) | copy-start | bytes 196612
  172.3 5.9 %collective-permute-start.2 = (f32[3,2560]{1,0:T(4,128)S(1)}, f32[3,2560]{1,0:T(4,128)S(1)}, u32[]{:S(2)}, u32[]{:S(2)}) collective-permute-start(f32[3,2560]{1,0:T(4,128)S(1)} %pad_maximum_fusion.1), channel_id=1, source_target_pairs={{2,0},{4,2},{6,4},{8,6},{10,8},{12,10},{14,12},{3,1},{5,3},{7,5},{... | collective-permute-start | bytes 92168 | tf_op jit(solution)/shard_map/ppermute | solution.py:274
  (48 other events, 159.1 us)
